TPU v7x, 32 devices: a whole 2x2x4 slice. The times are simulated.
32 devices in a mesh: space: 8 (over y, x, core), vec: 4 (over z).
Axes of the slice: x: 2, y: 2, z: 4, core: 2. Of those that a mesh axis runs over, the one named last changes fastest.
Arguments:
- vectors: float32 [2, 3, 384, 8, 2048], P(None, None, 'vec', 'space'), may hold values from -0.375 to 0.375
- links: float32 [3, 2, 3, 3, 8, 2048], P(None, None, None, None, 'space'), may hold values from -3.5 to 3.5
- momenta: int32 [2, 3], replicated, may hold values from -2 to 2
- directions: int32 [3], replicated, may hold values from 0 to 2, each once
Outputs:
- elementals: float32 [2, 3, 2, 384, 384], P(None, None, None, 'space', 'vec')
Inputs may be any that keep to these rules, and one draw needn't show every extreme that they name: directions holds each of 0, 1, 2 once.
All inputs are finite; a program needn't handle non-finite values.
Results may differ from a plain program's by a relative error of at most 0.000098.
Values sent between devices are 32-bit elements; how exact they have to be, the bound alone decides.
No kernel may reach another device: no remote copies, remote signals or barrier semaphores. Data moves between devices by JAX's collectives and lax.ppermute only.
A program may use at most 128 MiB of HBM per device.

v0:
```python
import jax
import jax.numpy as jnp
from jax import lax
from jax.sharding import PartitionSpec as P

LY = 32
LZ = 64


def padded_2(shard, sides, width):
    for axis, dim in sides:
        size, length = (lax.axis_size(axis), shard.shape[dim])
        up = [(i, (i + 1) % size) for i in range(size)]
        down = [(j, i) for i, j in up]
        last = lax.slice_in_dim(shard, length - width, length, axis=dim)
        first = lax.slice_in_dim(shard, 0, width, axis=dim)
        before = lax.ppermute(last, axis, up)
        after = lax.ppermute(first, axis, down)
        shard = jnp.concatenate([before, shard, after], axis=dim)
    return shard


def shifted(value, axis, steps):
    count = lax.axis_size(axis)
    pairs = [(source, (source + steps) % count) for source in range(count)]
    return lax.ppermute(value, axis, pairs)


def site_shift(field, mu, step, plane_y, plane_z):
    shape = field.shape
    cube = field.reshape(shape[:-1] + (plane_y, plane_z))
    cube = jnp.roll(cube, -step, axis=-3 + mu)
    return cube.reshape(shape)


def color_apply(link, field, dagger):
    link_re = link[0]
    link_im = link[1]
    if dagger:
        link_re = jnp.swapaxes(link_re, 0, 1)
        link_im = -jnp.swapaxes(link_im, 0, 1)
    link_re = link_re[:, :, None]
    link_im = link_im[:, :, None]
    field_re = field[0][None]
    field_im = field[1][None]
    out_re = jnp.sum(link_re * field_re - link_im * field_im, axis=1)
    out_im = jnp.sum(link_re * field_im + link_im * field_re, axis=1)
    return jnp.stack([out_re, out_im], 0)


def phase_tables(momenta, xcoord, sites, extent_x, plane_y, plane_z):
    ycoord = sites // plane_z
    zcoord = sites % plane_z
    p0 = momenta[:, 0][:, None, None]
    p1 = momenta[:, 1][:, None, None]
    p2 = momenta[:, 2][:, None, None]
    frac = (p0 * xcoord % extent_x).astype(jnp.float32) / extent_x
    frac = frac + (p1 * ycoord[None, None] % plane_y).astype(jnp.float32) / plane_y
    frac = frac + (p2 * zcoord[None, None] % plane_z).astype(jnp.float32) / plane_z
    theta = 2.0 * jnp.pi * frac
    return (jnp.cos(theta), jnp.sin(theta))


def elemental_block(left_vecs, right_disp, cosine, sine):
    vec_re = left_vecs[0][None]
    vec_im = left_vecs[1][None]
    cosine = cosine[:, None, None]
    sine = sine[:, None, None]
    left_re = vec_re * cosine - vec_im * sine
    left_im = -(vec_re * sine + vec_im * cosine)
    left = jnp.stack([left_re, left_im], 1)
    gram = jnp.einsum(
        "mpcaxs,dqcbxs->mpadqb",
        left,
        right_disp,
        precision=lax.Precision.HIGHEST,
        preferred_element_type=jnp.float32,
    )
    part_re = gram[:, 0, :, :, 0] - gram[:, 1, :, :, 1]
    part_im = gram[:, 0, :, :, 1] + gram[:, 1, :, :, 0]
    stacked = jnp.stack([part_re, part_im], 1)
    return jnp.transpose(stacked, (0, 3, 1, 2, 4))


def on_device(vectors, links, momenta, directions):
    plane_y = LY
    plane_z = LZ
    extent_x = lax.axis_size("space")
    xcoord = lax.axis_index("space")
    padded = padded_2(vectors, (("space", 3),), 1)
    lower = shifted(links[0], "space", 1)
    forward_x = color_apply(links[0], padded[:, :, :, 2:3], False)
    backward_x = color_apply(lower, padded[:, :, :, 0:1], True)
    displaced_list = [forward_x - backward_x]
    for mu in (1, 2):
        forward = color_apply(links[mu], site_shift(vectors, mu, 1, plane_y, plane_z), False)
        backward = site_shift(color_apply(links[mu], vectors, True), mu, -1, plane_y, plane_z)
        displaced_list.append(forward - backward)
    displaced = jnp.stack(displaced_list, 0)
    site_count = vectors.shape[4]
    sites = jnp.arange(site_count, dtype=jnp.int32)
    cosine, sine = phase_tables(momenta, xcoord, sites, extent_x, plane_y, plane_z)
    block = elemental_block(
        lax.all_gather(vectors, "vec", axis=2, tiled=True), displaced, cosine, sine
    )
    reduced = lax.psum_scatter(block, "space", scatter_dimension=3, tiled=True)
    return jnp.take(reduced, directions, axis=1)


def solution(mesh):
    placed = (
        P(None, None, "vec", "space", None),
        P(None, None, None, None, "space", None),
        P(),
        P(),
    )
    return jax.shard_map(
        on_device,
        mesh=mesh,
        in_specs=placed,
        out_specs=P(None, None, None, "space", "vec"),
        check_vma=False,
    )
```

profile of v0, /device:TPU:0, one launch (start us, length us, event | category | flops | bytes accessed | tf_op | source)
XLA Modules:
  0.0 521.4 jit_solution(13569363760980879944)
XLA Ops:
  7.3 3.4 collective-permute-start
  11.4 12.0 %copy.49 = f32[2,3,96,1,2048]{2,4,1,0,3:T(8,128)} copy(f32[2,3,96,1,2048]{4,3,2,1,0:T(1,128)} %param.4) | data formatting | bytes 9437184 | tf_op args[0]
  23.4 7.3 %slice.189 = f32[2,3,96,1,31,64]{2,5,4,1,0,3:T(8,128)} slice(f32[2,3,96,1,32,64]{2,5,4,1,0,3:T(8,128)} %bitcast.133), slice={[0:2], [0:3], [0:96], [0:1], [1:32], [0:64]} | slice | bytes 9142272 | tf_op jit(solution)/shard_map/jit(_roll_static)/slice | solution.py:32
  30.8 3.9 slice.193
  36.2 3.6 fusion.41
  42.0 11.1 %subtract_reduce_fusion.2 = (f32[3,96,2048]{2,1,0:T(8,128)}, f32[3,96,2048]{2,1,0:T(8,128)}, f32[3,96,2048]{2,1,0:T(8,128)}, f32[3,96,2048]{2,1,0:T(8,128)}) fusion(f32[3,96,2048]{2,1,0:T(8,128)S(1)} %get-tuple-element.50, f32[3,3,2048]{2,1,0:T(4,128)S(1)} %get-tuple-element.60, f32[3,96,2048]{2,1,0:T(8,128)S(1)} %get-tuple-element.51, ...), kind=kLoop, calls=%fused_computation.19 | loop fusion | flops 25952256 | bytes 14450688 | tf_op jit(solution)/shard_map/reduce_sum | solution.py:46
  55.4 3.6 copy.55
  59.0 6.9 %fusion.10 = (f32[1,3,96,1,32,64]{2,5,4,1,0,3:T(8,128)}, f32[1,3,96,1,32,64]{2,5,4,1,0,3:T(8,128)}) fusion(f32[2,3,96,1,31,64]{2,5,4,1,0,3:T(8,128)} %slice.189, f32[2,3,96,1,1,64]{2,5,4,1,0,3:T(8,128)S(1)} %slice.190), kind=kLoop, calls=%fused_computation.40 | loop fusion | flops 1179648 | bytes 9437184 | tf_op jit(solution)/shard_map/jit(_roll_static)/concatenate | solution.py:32
  65.9 3.4 copy.50
  69.3 3.4 copy.51
  72.7 3.5 copy.61
  76.2 3.5 copy.62
  79.7 7.0 %fusion.9 = (f32[1,3,96,1,32,64]{2,5,4,1,0,3:T(8,128)}, f32[1,3,96,1,32,64]{2,5,4,1,0,3:T(8,128)}) fusion(f32[2,3,96,1,32,63]{2,5,4,1,0,3:T(8,128)} %slice.193, f32[2,3,96,1,32,1]{2,5,4,1,0,3:T(1,128)S(1)} %slice.194), kind=kLoop, calls=%fused_computation.39 | loop fusion | flops 1179648 | bytes 9437184 | tf_op jit(solution)/shard_map/jit(_roll_static)/concatenate | solution.py:32
  86.7 3.4 copy.57
  90.1 3.4 copy.58
  93.7 5.2 %fusion.8 = f32[2,3,96,1,32,64]{2,5,4,1,3,0:T(8,128)} fusion(f32[1,3,96,1,32,64]{2,5,4,1,3,0:T(8,128)} %bitcast.142, f32[1,3,96,1,32,64]{2,5,4,1,3,0:T(8,128)S(1)} %bitcast.141), kind=kLoop, calls=%fused_computation.30 | loop fusion | flops 3538944 | bytes 9437184 | tf_op jit(solution)/shard_map/jit(_roll_static)/concatenate | solution.py:32
  99.8 3.7 fusion.7
  104.3 3.9 subtract_reduce_fusion.3
  108.3 4.7 subtract_reduce_fusion.1
  113.0 6.2 %copy.56 = f32[1,2,3,96,1,2048]{5,3,2,1,0,4:T(8,128)} copy(f32[1,2,3,96,1,2048]{3,5,2,1,4,0:T(8,128)} %bitcast.139) | data formatting | bytes 9437184 | tf_op jit(solution)/shard_map/reshape | solution.py:33
  119.2 6.6 %copy.63 = f32[1,2,3,96,1,2048]{5,3,2,1,0,4:T(8,128)} copy(f32[1,2,3,96,1,2048]{3,5,2,1,4,0:T(8,128)} %bitcast.140) | data formatting | bytes 9437184 | tf_op jit(solution)/shard_map/reshape | solution.py:33
  125.8 6.5 %maximum_subtract_fusion.1 = f32[1,2,3,96,1,2048]{5,3,2,1,0,4:T(8,128)} fusion(f32[1,2,3,96,1,2048]{5,3,2,1,0,4:T(8,128)} %copy.56, f32[1,1,3,96,1,2048]{5,3,2,1,0,4:T(8,128)} %bitcast.152, f32[1,1,3,96,1,2048]{5,3,2,1,0,4:T(8,128)S(1)} %bitcast.151), kind=kLoop, calls=%fused_computation.37 | loop fusion | flops 2359296 | bytes 14155776 | tf_op jit(solution)/shard_map/sub | solution.py:98
  132.9 3.0 maximum_subtract_fusion.2
  137.4 6.4 %fusion.40 = (f32[1,3,96,1,2048]{4,3,2,1,0:T(1,128)S(1)}, f32[1,3,96,1,2048]{4,3,2,1,0:T(1,128)S(1)}) fusion(f32[2,3,96,1,2048]{4,3,2,1,0:T(1,128)} %collective-permute-done), kind=kLoop, calls=%fused_computation.124 | loop fusion | bytes 9437184 | tf_op jit(solution)/shard_map/slice | solution.py:44
  148.9 6.4 %fusion.39 = (f32[1,3,96,1,2048]{4,3,2,1,0:T(1,128)S(1)}, f32[1,3,96,1,2048]{4,3,2,1,0:T(1,128)S(1)}) fusion(f32[2,3,96,1,2048]{4,3,2,1,0:T(1,128)} %collective-permute-done.2), kind=kLoop, calls=%fused_computation.123 | loop fusion | bytes 9437184 | tf_op jit(solution)/shard_map/slice | solution.py:44
  163.2 170.9 %all-gather.2.cloned.1.call-done = f32[2,3,384,1,2048]{4,3,2,1,0:T(1,128)} async-done(((f32[2,3,96,1,2048]{4,3,2,1,0:T(1,128)}), f32[2,3,384,1,2048]{4,3,2,1,0:T(1,128)}) %all-gather.2.cloned.1.call-update) | async-done | bytes 18874384 | tf_op jit(solution)/shard_map/all_gather | solution.py:104
  334.1 13.3 %fusion.38 = (f32[1,3,384,1,2048]{4,3,2,1,0:T(1,128)}, f32[1,3,384,1,2048]{4,3,2,1,0:T(1,128)}) fusion(f32[2,3,384,1,2048]{4,3,2,1,0:T(1,128)} %all-gather.2.cloned.1.call-done), kind=kLoop, calls=%fused_computation.122 | loop fusion | bytes 37748736 | tf_op jit(solution)/shard_map/slice | solution.py:65
  347.3 13.7 %copy_bitcast_fusion = (f32[3,384,2048]{2,1,0:T(8,128)S(1)}, f32[3,384,2048]{2,1,0:T(8,128)S(1)}) fusion(f32[1,3,384,1,2048]{4,3,2,1,0:T(1,128)} %get-tuple-element.25, f32[1,3,384,1,2048]{4,3,2,1,0:T(1,128)} %get-tuple-element.24), kind=kLoop, calls=%fused_computation.12 | loop fusion | bytes 37748736
  361.0 13.2 %multiply_subtract_fusion = (f32[2,1,3,384,1,2048]{5,3,2,1,0,4:T(8,128)}, f32[2,1,3,384,1,2048]{5,3,2,1,0,4:T(8,128)}) fusion(f32[2,2048]{1,0:T(2,128)S(1)} %get-tuple-element.49, f32[3,384,2048]{2,1,0:T(8,128)S(1)} %get-tuple-element.70, f32[2,2048]{1,0:T(2,128)S(1)} %get-tuple-element.48, f32[3,384,2048]{2,1,0:T(8,128)S(1)} %get-tuple-element.71), kind=kLoop, calls=%fused_computation.6 | loop fusion | flops 33030144 | bytes 56655872 | tf_op jit(solution)/shard_map/sub | solution.py:69
  374.2 71.7 %fusion.11 = f32[2,2,384,3,2,96]{2,5,4,3,1,0:T(8,128)S(1)} fusion(f32[1,2,3,96,1,2048]{5,3,2,1,0,4:T(8,128)} %maximum_subtract_fusion.2, f32[1,2,3,96,1,2048]{5,3,2,1,0,4:T(8,128)} %maximum_subtract_fusion.1, f32[1,2,3,96,1,2048]{5,3,2,1,0,4:T(8,128)} %maximum_subtract_fusion, f32[2,1,3,384,1,2048]{5,3,2,1,0,4:T(8,128)} %get-tuple-element.23, ...), kind=kOutput, calls=%fused_computation.49 | convolution fusion | flops 65246330880 | bytes 55443456 | tf_op jit(solution)/shard_map/mpcaxs,dqcbxs->mpadqb/dot_general | solution.py:72
  446.3 3.1 copy.66
  450.7 60.5 %all-reduce.3.cloned.1.call-done = f32[2,3,2,384,96]{4,2,1,0,3:T(2,128)} async-done(((f32[2,3,2,384,96]{4,2,1,0,3:T(2,128)}), f32[2,3,2,384,96]{4,2,1,0,3:T(2,128)}) %all-reduce.3.cloned.1.call-update) | async-done | bytes 1769488
  (85 shorter events, 28.0 us)
Async XLA Ops:
  6.5 4.2 copy-start.10
  6.5 327.5 %all-gather.2.cloned.1.call-start = ((), (), s32[]{:S(2)}) async-start(), calls=%async_computation | async-start | bytes 23592960 | tf_op jit(solution)/shard_map/all_gather | solution.py:104
  7.3 504.0 %all-reduce.3.cloned.1.call-start = ((), (), s32[]{:S(2)}) async-start(), calls=%async_computation.1 | async-start | bytes 4718592
  7.3 130.1 %collective-permute-start = (f32[2,3,96,1,2048]{4,3,2,1,0:T(1,128)}, f32[2,3,96,1,2048]{4,3,2,1,0:T(1,128)}, u32[]{:S(2)}, u32[]{:S(2)}) collective-permute-start(f32[2,3,96,1,2048]{4,3,2,1,0:T(1,128)} %param.4), channel_id=1, source_target_pairs={{4,0},{8,4},{12,8},{16,12},{20,16},{24,20},{28,24},{0,28},{5,1},{9... | collective-permute-start | bytes 14155784 | tf_op jit(solution)/shard_map/ppermute | solution.py:18
  10.7 138.1 %collective-permute-start.2 = (f32[2,3,96,1,2048]{4,3,2,1,0:T(1,128)}, f32[2,3,96,1,2048]{4,3,2,1,0:T(1,128)}, u32[]{:S(2)}, u32[]{:S(2)}) collective-permute-start(f32[2,3,96,1,2048]{4,3,2,1,0:T(1,128)} %param.4), channel_id=1, source_target_pairs={{0,4},{4,8},{8,12},{12,16},{16,20},{20,24},{24,28},{28,0},{1,5},{5... | collective-permute-start | bytes 14155784 | tf_op jit(solution)/shard_map/ppermute | solution.py:17
  11.4 124.9 %collective-permute-start.1 = (f32[2,3,3,1,2048]{4,3,2,1,0:T(1,128)}, f32[2,3,3,1,2048]{4,3,2,1,0:T(1,128)}, u32[]{:S(2)}, u32[]{:S(2)}) collective-permute-start(f32[2,3,3,1,2048]{4,3,2,1,0:T(1,128)} %slice_bitcast_fusion.2), channel_id=1, source_target_pairs={{0,4},{4,8},{8,12},{12,16},{16,20},{20,24},{24,28},{28,0},{1,5},{5... | collective-permute-start | bytes 442376 | tf_op jit(solution)/shard_map/ppermute | solution.py:26
  23.4 7.3 %copy-start = (f32[2,3,96,1,2048]{2,4,1,0,3:T(8,128)S(1)}, f32[2,3,96,1,2048]{2,4,1,0,3:T(8,128)}, u32[]{:S(2)}) copy-start(f32[2,3,96,1,2048]{2,4,1,0,3:T(8,128)} %copy.49) | copy-start | bytes 14155780
  30.8 5.4 %slice-start = ((s8[4718592]{0:T(1024)(128)(4,1)}), s8[4194304]{0:T(1024)(128)(4,1)S(1)}, s32[]{:S(2)}) async-start(s8[4718592]{0:T(1024)(128)(4,1)} %bitcast.137), calls=%async_computation.2 | async-start | bytes 8388608
  30.8 5.4 %slice-start.1 = ((s8[4718592]{0:T(1024)(128)(4,1)}), s8[524288]{0:T(1024)(128)(4,1)S(1)}, s32[]{:S(2)}) async-start(s8[4718592]{0:T(1024)(128)(4,1)} %bitcast.137), calls=%async_computation.3 | async-start | bytes 1048576
  86.7 6.8 %copy-start.16 = (s32[2,3]{1,0:T(2,128)S(1)}, s32[2,3]{1,0:T(2,128)}, u32[]{:S(2)}) copy-start(s32[2,3]{1,0:T(2,128)} %param.6) | copy-start | bytes 76
  93.7 5.3 %copy-start.14 = (f32[1,1,3,3,1,2048]{5,4,3,2,1,0:T(1,128)S(1)}, f32[1,1,3,3,1,2048]{5,4,3,2,1,0:T(1,128)}, u32[]{:S(2)}) copy-start(f32[1,1,3,3,1,2048]{5,4,3,2,1,0:T(1,128)} %get-tuple-element.41) | copy-start | bytes 221188
  93.7 5.3 %copy-start.15 = (f32[1,1,3,3,1,2048]{5,4,3,2,1,0:T(1,128)S(1)}, f32[1,1,3,3,1,2048]{5,4,3,2,1,0:T(1,128)}, u32[]{:S(2)}) copy-start(f32[1,1,3,3,1,2048]{5,4,3,2,1,0:T(1,128)} %get-tuple-element.42) | copy-start | bytes 221188
  93.7 5.4 %copy-start.12 = (f32[1,1,3,3,1,2048]{5,4,3,2,1,0:T(1,128)S(1)}, f32[1,1,3,3,1,2048]{5,4,3,2,1,0:T(1,128)}, u32[]{:S(2)}) copy-start(f32[1,1,3,3,1,2048]{5,4,3,2,1,0:T(1,128)} %get-tuple-element.44) | copy-start | bytes 221188
  93.7 5.4 %copy-start.13 = (f32[1,1,3,3,1,2048]{5,4,3,2,1,0:T(1,128)S(1)}, f32[1,1,3,3,1,2048]{5,4,3,2,1,0:T(1,128)}, u32[]{:S(2)}) copy-start(f32[1,1,3,3,1,2048]{5,4,3,2,1,0:T(1,128)} %get-tuple-element.45) | copy-start | bytes 221188
  93.7 5.5 %copy-start.2 = (f32[3,96,2048]{1,2,0:T(8,128)S(1)}, f32[3,96,2048]{1,2,0:T(8,128)}, u32[]{:S(2)}) copy-start(f32[3,96,2048]{1,2,0:T(8,128)} %copy.61) | copy-start | bytes 7077892
  93.7 6.0 %copy-start.3 = (f32[3,96,2048]{1,2,0:T(8,128)S(1)}, f32[3,96,2048]{1,2,0:T(8,128)}, u32[]{:S(2)}) copy-start(f32[3,96,2048]{1,2,0:T(8,128)} %copy.62) | copy-start | bytes 7077892
  99.8 3.7 copy-start.11
  99.8 3.8 copy-start.6
  99.8 4.6 copy-start.7
  104.3 3.9 copy-start.8
  104.3 3.9 copy-start.9
  125.8 6.6 %copy-start.1 = (f32[1,2,3,96,1,2048]{5,3,2,1,0,4:T(8,128)S(1)}, f32[1,2,3,96,1,2048]{5,3,2,1,0,4:T(8,128)}, u32[]{:S(2)}) copy-start(f32[1,2,3,96,1,2048]{5,3,2,1,0,4:T(8,128)} %copy.63) | copy-start | bytes 14155780
  125.8 6.6 %copy-start.4 = (f32[3,96,2048]{2,1,0:T(8,128)S(1)}, f32[3,96,2048]{2,1,0:T(8,128)}, u32[]{:S(2)}) copy-start(f32[3,96,2048]{2,1,0:T(8,128)} %get-tuple-element.13) | copy-start | bytes 7077892
  125.8 7.1 %copy-start.5 = (f32[3,96,2048]{2,1,0:T(8,128)S(1)}, f32[3,96,2048]{2,1,0:T(8,128)}, u32[]{:S(2)}) copy-start(f32[3,96,2048]{2,1,0:T(8,128)} %get-tuple-element.14) | copy-start | bytes 7077892
  446.1 3.3 copy-start.18
  446.1 4.6 copy-start.17
Sparse Core Ops, SparseCore 0:
  8.9 325.1 all-gather.1
  449.6 61.6 all-reduce.2
where the time goes:
time: 531 us; the launch traced here: 521 us
  waiting for transfers between devices  232 us (44%)
  local copies, waits for them, and re-layouts  122 us (23%)
  other arithmetic  77.1 us (15%)
  matrix products  71.7 us (14%)
  between operations  14.8 us (3%)
    all_gather x1, waiting for transfers between devices, on_device(): lax.all_gather(vectors, 'vec', axis=2, tiled=True)  171 us
    dot_general x1, matrix products, elemental_block(): jnp.einsum('mpcaxs,dqcbxs->mpadqb', left, right_disp, precision=lax.Preci...  71.7 us
    unnamed x3, waiting for transfers between devices  61.3 us
    unnamed x52, local copies, waits for them, and re-layouts  36.2 us
    reduce_sum x5, other arithmetic, color_apply(): out_re = jnp.sum(link_re * field_re - link_im * field_im, axis=1)  25.2 us
    concatenate x4, other arithmetic, site_shift(): cube = jnp.roll(cube, -step, axis=-3 + mu)  22.9 us
    slice x3, local copies, waits for them, and re-layouts, color_apply(): field_re = field[0][None]  16.5 us
    mul x7, local copies, waits for them, and re-layouts, color_apply(): out_re = jnp.sum(link_re * field_re - link_im * field_im, axis=1)  13.8 us
  transfers between devices with their start and end apart: 5, of which 2 were waited for; matrix products, arithmetic and copies ran while one was open for 29% of the time, Pallas kernels for 0%

commit v1 on v0

v1 whole, which is shorter than its diff:
```python
import functools

import jax
import jax.numpy as jnp
from jax import lax
from jax.experimental import pallas as pl
from jax.experimental.pallas import tpu as pltpu
from jax.sharding import PartitionSpec as P

LANES = 128
PLANE_Z = 64
TILE = 16
F32 = jnp.float32
BF16 = jnp.bfloat16


def xor_pairs(size, k):
    return [(i, i ^ k) for i in range(size)]


def bits_of(size):
    return size.bit_length() - 1


def split(value):
    high = value.astype(BF16)
    return high, (value - high.astype(F32)).astype(BF16)


def matvec(link, re, im, dagger):
    out_re, out_im = [], []
    for row in range(3):
        acc_re = acc_im = None
        for col in range(3):
            u_re, u_im = link[col * 3 + row] if dagger else link[row * 3 + col]
            if dagger:
                t_re = u_re * re[col] + u_im * im[col]
                t_im = u_re * im[col] - u_im * re[col]
            else:
                t_re = u_re * re[col] - u_im * im[col]
                t_im = u_re * im[col] + u_im * re[col]
            acc_re = t_re if acc_re is None else acc_re + t_re
            acc_im = t_im if acc_im is None else acc_im + t_im
        out_re.append(acc_re)
        out_im.append(acc_im)
    return out_re, out_im


def chunk_kernel(has_acc, nv, coef_ref, v_ref, vx_ref, row_ref, *refs):
    if has_acc:
        acc_ref, out_ref, left_v, left_w, left_r, right, right_r = refs
    else:
        out_ref, left_v, left_w, left_r, right, right_r = refs
        acc_ref = None

    @pl.when(pl.program_id(0) == 0)
    def _():
        lane = lax.broadcasted_iota(jnp.int32, (TILE, LANES), 1)
        low = lane < PLANE_Z
        at_end = lane % PLANE_Z == PLANE_Z - 1
        at_start = lane % PLANE_Z == 0

        def coef(index):
            return jnp.broadcast_to(coef_ref[pl.ds(index, 1), :], (TILE, LANES))

        def link_of(mu):
            return [
                (coef(mu * 18 + e), coef(mu * 18 + 9 + e)) for e in range(9)
            ]

        def put(ref, rows, col, value):
            high, rest = split(value)
            ref[0, rows, pl.ds(col * LANES, LANES)] = high
            ref[1, rows, pl.ds(col * LANES, LANES)] = rest

        def phased(ref, rows_of, re, im, base):
            for m in range(2):
                cos, sin = coef(base + 2 * m), coef(base + 2 * m + 1)
                for c in range(3):
                    p = re[c] * cos - im[c] * sin
                    q = re[c] * sin + im[c] * cos
                    p_hi, p_lo = split(p)
                    q_hi, q_lo = split(q)
                    for half, (pp, qq) in enumerate(((p_hi, q_hi), (p_lo, q_lo))):
                        ref[half, rows_of(2 * m), pl.ds(c * LANES, LANES)] = pp
                        ref[half, rows_of(2 * m), pl.ds((3 + c) * LANES, LANES)] = qq
                        ref[half, rows_of(2 * m + 1), pl.ds(c * LANES, LANES)] = -qq
                        ref[half, rows_of(2 * m + 1), pl.ds((3 + c) * LANES, LANES)] = pp

        def body(step, carry):
            start = pl.multiple_of(step * TILE, TILE)
            rows = pl.ds(start, TILE)

            def rows_of(part):
                return pl.ds(pl.multiple_of(part * nv + start, TILE), TILE)

            re = [v_ref[c, rows, :] for c in range(3)]
            im = [v_ref[3 + c, rows, :] for c in range(3)]
            phased(left_v, rows_of, re, im, 54)
            xre = [vx_ref[c, rows, :] for c in range(3)]
            xim = [vx_ref[3 + c, rows, :] for c in range(3)]
            wre, wim = matvec(link_of(0), xre, xim, False)
            phased(left_w, rows_of, wre, wim, 58)
            for c in range(3):
                put(right.at[0], rows, c, wre[c])
                put(right.at[0], rows, 3 + c, wim[c])
                put(right.at[3], rows, c, re[c])
                put(right.at[3], rows, 3 + c, im[c])
            packed = [row_ref[c, rows, :] for c in range(3)]
            turned = [pltpu.roll(packed[c], PLANE_Z, 1) for c in range(3)]
            link1 = link_of(1)
            fre = [jnp.where(low, pltpu.roll(re[c], PLANE_Z, 1), turned[c]) for c in range(3)]
            fim = [jnp.where(low, pltpu.roll(im[c], PLANE_Z, 1), packed[c]) for c in range(3)]
            fre, fim = matvec(link1, fre, fim, False)
            bre, bim = matvec(link1, re, im, True)
            for c in range(3):
                r_re = pltpu.roll(bre[c], PLANE_Z, 1)
                r_im = pltpu.roll(bim[c], PLANE_Z, 1)
                put(right.at[1], rows, c, jnp.where(low, fre[c], fre[c] - r_re))
                put(right.at[1], rows, 3 + c, jnp.where(low, fim[c], fim[c] - r_im))
                put(right_r, rows, c, -jnp.where(low, r_re, bim[c]))
            for part in range(4):
                a, b = coef(62 + 2 * part), coef(63 + 2 * part)
                for c in range(3):
                    n_re = jnp.where(low, packed[c], turned[c])
                    n_im = jnp.where(low, turned[c], packed[c])
                    put(left_r, rows_of(part), c, n_re * a + n_im * b)
            link2 = link_of(2)
            zre = [jnp.where(at_end, pltpu.roll(re[c], PLANE_Z - 1, 1), pltpu.roll(re[c], LANES - 1, 1)) for c in range(3)]
            zim = [jnp.where(at_end, pltpu.roll(im[c], PLANE_Z - 1, 1), pltpu.roll(im[c], LANES - 1, 1)) for c in range(3)]
            zre, zim = matvec(link2, zre, zim, False)
            bre, bim = matvec(link2, re, im, True)
            for c in range(3):
                r_re = jnp.where(at_start, pltpu.roll(bre[c], PLANE_Z + 1, 1), pltpu.roll(bre[c], 1, 1))
                r_im = jnp.where(at_start, pltpu.roll(bim[c], PLANE_Z + 1, 1), pltpu.roll(bim[c], 1, 1))
                put(right.at[2], rows, c, zre[c] - r_re)
                put(right.at[2], rows, 3 + c, zim[c] - r_im)
            return carry

        lax.fori_loop(0, nv // TILE, body, 0)

    part = pl.program_id(0)
    rows = pl.ds(pl.multiple_of(part * nv, nv), nv)

    def product(left, right_side):
        dims = (((1,), (1,)), ((), ()))
        total = None
        for i, j in ((0, 0), (0, 1), (1, 0)):
            term = lax.dot_general(
                left[i, rows, :], right_side[j], dims, preferred_element_type=F32
            )
            total = term if total is None else total + term
        return total

    for mu in range(3):
        total = product(left_v, right.at[mu])
        if mu == 0:
            total = total + product(left_w, right.at[3])
        if mu == 1:
            total = total + product(left_r, right_r)
        if has_acc:
            total = total + acc_ref[mu]
        out_ref[mu] = total


def chunk_call(coef, v, vx, row, acc):
    nv = v.shape[1]
    has_acc = acc is not None
    whole = lambda shape: pl.BlockSpec(shape, lambda i: (0,) * len(shape))
    tile = pl.BlockSpec((3, nv, nv), lambda i: (0, i, 0))
    args = [coef, v, vx, row] + ([acc] if has_acc else [])
    specs = [whole(a.shape) for a in args[:4]] + ([tile] if has_acc else [])
    wide = 6 * LANES
    flops = 3 * 2 * 4 * nv * nv * wide * 4
    return pl.pallas_call(
        functools.partial(chunk_kernel, has_acc, nv),
        out_shape=jax.ShapeDtypeStruct((3, 4 * nv, nv), F32),
        grid=(4,),
        in_specs=specs,
        out_specs=tile,
        scratch_shapes=[
            pltpu.VMEM((2, 4 * nv, wide), BF16),
            pltpu.VMEM((2, 4 * nv, wide), BF16),
            pltpu.VMEM((2, 4 * nv, wide // 2), BF16),
            pltpu.VMEM((4, 2, nv, wide), BF16),
            pltpu.VMEM((2, nv, wide // 2), BF16),
        ],
        input_output_aliases={4: 0} if has_acc else {},
        cost_estimate=pl.CostEstimate(
            flops=flops, bytes_accessed=24 * nv * nv, transcendentals=0
        ),
        compiler_params=pltpu.CompilerParams(vmem_limit_bytes=56 * 1024 * 1024),
        name="chunk",
    )(*args)


def phase_rows(momenta, xcoord, sites, extent_x, plane_y):
    ycoord = sites // PLANE_Z
    zcoord = sites % PLANE_Z
    p0, p1, p2 = (momenta[:, i][:, None] for i in range(3))
    frac = (p0 * xcoord % extent_x).astype(F32) / extent_x
    frac = frac + (p1 * ycoord[None] % plane_y).astype(F32) / plane_y
    frac = frac + (p2 * zcoord[None] % PLANE_Z).astype(F32) / PLANE_Z
    theta = 2.0 * jnp.pi * frac
    return jnp.cos(theta), jnp.sin(theta)


def coefficients(links, momenta, xcoord, start, subs, extent_x, plane):
    plane_y = plane // PLANE_Z
    width = subs * LANES
    rows = lax.dynamic_slice_in_dim(links.reshape(54, plane), start, width, 1)
    sites = start + jnp.arange(width, dtype=jnp.int32)
    cos, sin = phase_rows(momenta, xcoord, sites, extent_x, plane_y)
    cos_x, sin_x = phase_rows(momenta, xcoord + 1, sites, extent_x, plane_y)
    after = jnp.arange(subs, dtype=jnp.int32)[:, None] * LANES + LANES
    after = start + after + jnp.arange(LANES, dtype=jnp.int32)[None] % PLANE_Z
    cos_r, sin_r = phase_rows(
        momenta, xcoord, after.reshape(-1) % plane, extent_x, plane_y
    )
    low = jnp.arange(width) % LANES < PLANE_Z
    parts = [rows]
    for m in range(2):
        parts += [cos[m : m + 1], sin[m : m + 1]]
    for m in range(2):
        parts += [-cos_x[m : m + 1], -sin_x[m : m + 1]]
    for m in range(2):
        c, s = cos_r[m : m + 1], sin_r[m : m + 1]
        parts += [
            jnp.where(low, c, s),
            jnp.where(low, -s, c),
            jnp.where(low, -s, c),
            jnp.where(low, -c, -s),
        ]
    parts.append(jnp.zeros((2, width), F32))
    table = jnp.concatenate(parts, 0)
    return [table[:, i * LANES : (i + 1) * LANES] for i in range(subs)]


def scatter_step(value, axis_dim, mine, axis, bit, size):
    keep = lax.dynamic_index_in_dim(value, mine, axis_dim, keepdims=False)
    send = lax.dynamic_index_in_dim(value, 1 - mine, axis_dim, keepdims=False)
    return keep + lax.ppermute(send, axis, xor_pairs(size, bit))


def reduce_block(block, order, n_space, n_vec):
    s = lax.axis_index("space")
    t = lax.axis_index("vec")
    s_bits, v_bits = bits_of(n_space), bits_of(n_vec)
    nv = block.shape[1]
    value = block.reshape((4,) + (2,) * s_bits + (nv // n_space, nv))
    left = list(range(s_bits))
    for level in order:
        mine = (s >> (s_bits - 1 - level)) & 1
        if level < v_bits:
            mine = mine ^ ((t >> (v_bits - 1 - level)) & 1)
        value = scatter_step(
            value, 1 + left.index(level), mine, "space", 1 << (s_bits - 1 - level), n_space
        )
        left.remove(level)
    width = nv // n_vec
    value = value.reshape(4, nv // n_space, n_vec, width)
    total = value[:, :, 0]
    for k in range(1, n_vec):
        total = total + lax.ppermute(value[:, :, k], "vec", xor_pairs(n_vec, k))
    return total


def on_device(vectors, links, momenta, directions):
    n_space, n_vec = lax.axis_size("space"), lax.axis_size("vec")
    s, t = lax.axis_index("space"), lax.axis_index("vec")
    own = vectors.shape[2]
    plane = vectors.shape[4]
    chunk = plane // n_vec
    subs = chunk // LANES
    field = vectors.reshape(6, own, plane)
    down = [(i, (i - 1) % n_space) for i in range(n_space)]

    def piece(k, sub):
        start = (t ^ k) * chunk + sub * LANES
        return lax.dynamic_slice_in_dim(field, start, LANES, 2)

    def first_row(k):
        start = (((t ^ k) + 1) % n_vec) * chunk
        row = lax.dynamic_slice_in_dim(field, start, PLANE_Z, 2)
        return jnp.concatenate([row[:3], row[3:]], 2)

    gather = lambda part: jnp.concatenate(
        [part(0)] + [lax.ppermute(part(k), "vec", xor_pairs(n_vec, k)) for k in range(1, n_vec)],
        1,
    )
    row = gather(first_row)
    tables = coefficients(links, momenta, s, t * chunk, subs, n_space * vectors.shape[3], plane)
    acc = None
    for sub in reversed(range(subs)):
        v = gather(lambda k: piece(k, sub))
        vx = lax.ppermute(v, "space", down)
        acc = chunk_call(tables[sub], v, vx, row, acc)
        row = jnp.concatenate([v[:3, :, :PLANE_Z], v[3:, :, :PLANE_Z]], 2)
    nv = own * n_vec
    s_bits = bits_of(n_space)
    forward = list(reversed(range(s_bits)))
    outs = []
    for mu in range(3):
        order = forward if mu != 1 else forward[:1] + list(reversed(forward[1:]))
        outs.append(reduce_block(acc[mu].reshape(4, nv, nv), order, n_space, n_vec))
    out = jnp.stack(outs, 0)
    out = jnp.take(out, directions, axis=0)
    out = out.reshape((3, 2, 2) + out.shape[2:])
    return jnp.transpose(out, (1, 0, 2, 3, 4))


def solution(mesh):
    placed = (
        P(None, None, "vec", "space", None),
        P(None, None, None, None, "space", None),
        P(),
        P(),
    )
    return jax.shard_map(
        on_device,
        mesh=mesh,
        in_specs=placed,
        out_specs=P(None, None, None, "space", "vec"),
        check_vma=False,
    )
```

time: 531 us -> 316 us (0.60); the launches traced: 521 us -> 315 us
  waiting for transfers between devices: 232 us -> 75.5 us
  Pallas kernels: 0 us -> 109 us
  local copies, waits for them, and re-layouts: 122 us -> 29.9 us
  starting transfers between devices: 3.46 us -> 85.1 us
  matrix products: 71.7 us -> 0 us
  other arithmetic: 77.1 us -> 15.7 us
  between operations: 14.8 us -> 0.53 us
    all_gather x1 -> x0, waiting for transfers between devices: 171 us -> none  [on_device(): lax.all_gather(vectors, 'vec', axis=2, tiled=True)]
    pallas_call x0 -> x4, Pallas kernels: none -> 109 us  [chunk_call(): pl.pallas_call(functools.partial(chunk_kernel, has_acc, nv), out_shape=ja...]
    ppermute x3 -> x37, starting transfers between devices: 3.42 us -> 85.1 us  [the longest x15 49.7 us: on_device(): lax.ppermute(part(k), 'vec', xor_pairs(n_vec, k))]
    ppermute x3 -> x37, waiting for transfers between devices: 0.01 us -> 75.5 us  [the longest x15 48.4 us: on_device(): lax.ppermute(part(k), 'vec', xor_pairs(n_vec, k))]
    dot_general x1 -> x0, matrix products: 71.7 us -> none  [elemental_block(): jnp.einsum('mpcaxs,dqcbxs->mpadqb', left, right_disp, precision=lax.Preci...]
    unnamed x3 -> x0, waiting for transfers between devices: 61.3 us -> none
    slice x8 -> x12, local copies, waits for them, and re-layouts: 41 us -> 8.4 us  [the longest x1 3.55 us: on_device(): outs.append(reduce_block(acc[mu].reshape(4, nv, nv), order, n_space, n_vec))]
    sub x5 -> x0, other arithmetic: 25.9 us -> none  [the longest x1 13.2 us: elemental_block(): left_re = vec_re * cosine - vec_im * sine]
  transfers between devices with their start and end apart: 5 -> 37, of which waited for: 2 -> 11; matrix products, arithmetic and copies ran while one was open for 29% -> 8% of each run, Pallas kernels for 0% -> 26%
where the time goes in v1:
time: 316 us; the launch traced here: 315 us
  Pallas kernels  109 us (34%)
  starting transfers between devices  85.1 us (27%)
  waiting for transfers between devices  75.5 us (24%)
  local copies, waits for them, and re-layouts  29.9 us (9%)
  other arithmetic  15.7 us (5%)
    pallas_call x4, Pallas kernels, chunk_call(): pl.pallas_call(functools.partial(chunk_kernel, has_acc, nv), out_shape=ja...  109 us
    ppermute x15, starting transfers between devices, on_device(): lax.ppermute(part(k), 'vec', xor_pairs(n_vec, k))  49.7 us
    ppermute x15, waiting for transfers between devices, on_device(): lax.ppermute(part(k), 'vec', xor_pairs(n_vec, k))  48.4 us
    ppermute x9, starting transfers between devices, reduce_block(): total = total + lax.ppermute(value[:, :, k], 'vec', xor_pairs(n_vec, k))  22.7 us
    ppermute x9, waiting for transfers between devices, scatter_step(): return keep + lax.ppermute(send, axis, xor_pairs(size, bit))  20.3 us
    unnamed x29, local copies, waits for them, and re-layouts  11.8 us
    ppermute x9, starting transfers between devices, scatter_step(): return keep + lax.ppermute(send, axis, xor_pairs(size, bit))  9.87 us
    ppermute x9, waiting for transfers between devices, reduce_block(): total = total + lax.ppermute(value[:, :, k], 'vec', xor_pairs(n_vec, k))  6.83 us
  transfers between devices with their start and end apart: 37, of which 11 were waited for; matrix products, arithmetic and copies ran while one was open for 8% of the time, Pallas kernels for 26%

profile of v1, /device:TPU:0, one launch (start us, length us, event | category | flops | bytes accessed | tf_op | source)
XLA Modules:
  0.0 315.3 jit_solution(624508976957638723)
XLA Ops:
  0.0 6.7 %copy.28 = f32[2,3,96,1,2048]{4,2,3,1,0:T(8,128)} copy(f32[2,3,96,1,2048]{4,3,2,1,0:T(1,128)} %param.4) | data formatting | bytes 9437184
  6.7 1.7 constant_dynamic-slice_fusion.3
  9.2 3.1 collective-permute-start.16
  13.1 2.6 collective-permute-start.17
  16.4 4.0 %constant_dynamic-slice_fusion.17 = (f32[6,96,128]{2,1,0:T(8,128)S(1)}, f32[6,96,128]{2,1,0:T(8,128)}, f32[6,96,128]{2,1,0:T(8,128)}, f32[6,96,128]{2,1,0:T(8,12...) fusion(f32[6,96,2048]{2,1,0:T(8,128)} %bitcast.95, ...), kind=kLoop, calls=%fused_computation.52 | loop fusion | bytes 9437248 | tf_op jit(solution)/shard_map/dynamic_slice | solution.py:280
  21.3 3.5 %collective-permute-start.13 = (f32[6,96,128]{2,1,0:T(8,128)}, f32[6,96,128]{2,1,0:T(8,128)}, u32[]{:S(2)}, u32[]{:S(2)}) collective-permute-start(f32[6,96,128]{2,1,0:T(8,128)} %get-tuple-element.22), channel_id=1, source_target_pairs={{0,2},{1,3},{2,0},{3,1},{4,6},{5,7},{6,4},{7,5},{8,10},{9,11},{10,... | collective-permute-start | bytes 884744 | tf_op jit(solution)/shard_map/ppermute | solution.py:288
  29.0 3.8 %collective-permute-start.10 = (f32[6,96,128]{2,1,0:T(8,128)}, f32[6,96,128]{2,1,0:T(8,128)S(1)}, u32[]{:S(2)}, u32[]{:S(2)}) collective-permute-start(f32[6,96,128]{2,1,0:T(8,128)} %get-tuple-element.24), channel_id=1, source_target_pairs={{0,3},{1,2},{2,1},{3,0},{4,7},{5,6},{6,5},{7,4},{8,11},{9,10},{10,... | collective-permute-start | bytes 884744 | tf_op jit(solution)/shard_map/ppermute | solution.py:288
  35.0 20.7 %collective-permute-done.13 = f32[6,96,128]{2,1,0:T(8,128)} collective-permute-done((f32[6,96,128]{2,1,0:T(8,128)}, f32[6,96,128]{2,1,0:T(8,128)}, u32[]{:S(2)}, u32[]{:S(2)}) %collective-permute-start.13) | collective-permute-done | bytes 294944 | tf_op jit(solution)/shard_map/ppermute | solution.py:288
  56.7 13.0 %collective-permute-start.5 = (f32[6,96,128]{2,1,0:T(8,128)}, f32[6,96,128]{2,1,0:T(8,128)S(1)}, u32[]{:S(2)}, u32[]{:S(2)}) collective-permute-start(f32[6,96,128]{2,1,0:T(8,128)} %get-tuple-element.29), channel_id=1, source_target_pairs={{0,2},{1,3},{2,0},{3,1},{4,6},{5,7},{6,4},{7,5},{8,10},{9,11},{10,... | collective-permute-start | bytes 884744 | tf_op jit(solution)/shard_map/ppermute | solution.py:288
  71.1 2.0 pad_maximum_fusion.7.row_ref
  73.1 18.1 %collective-permute-start = (f32[6,96,128]{2,1,0:T(8,128)S(1)}, f32[6,96,128]{2,1,0:T(8,128)S(1)}, u32[]{:S(2)}, u32[]{:S(2)}) collective-permute-start(f32[6,96,128]{2,1,0:T(8,128)S(1)} %get-tuple-element.34), channel_id=1, source_target_pairs={{0,1},{1,0},{2,3},{3,2},{4,5},{5,4},{6,7},{7,6},{8,9},{9,8},{10,11... | collective-permute-start | bytes 884744 | tf_op jit(solution)/shard_map/ppermute | solution.py:288
  91.2 2.4 collective-permute-done.9
  93.6 2.4 collective-permute-start.2
  97.2 15.3 %collective-permute-done.5 = f32[6,96,128]{2,1,0:T(8,128)S(1)} collective-permute-done((f32[6,96,128]{2,1,0:T(8,128)}, f32[6,96,128]{2,1,0:T(8,128)S(1)}, u32[]{:S(2)}, u32[]{:S(2)}) %collective-permute-start.5) | collective-permute-done | bytes 294944 | tf_op jit(solution)/shard_map/ppermute | solution.py:288
  112.5 2.6 collective-permute-start.11
  115.2 9.9 %collective-permute-done.1 = f32[6,96,128]{2,1,0:T(8,128)S(1)} collective-permute-done((f32[6,96,128]{2,1,0:T(8,128)S(1)}, f32[6,96,128]{2,1,0:T(8,128)S(1)}, u32[]{:S(2)}, u32[]{:S(2)}) %collective-permute-start.1) | collective-permute-done | bytes 294944 | tf_op jit(solution)/shard_map/ppermute | solution.py:288
  130.7 26.6 %chunk.4.refs_0_ = f32[3,1536,384]{2,1,0:T(8,128)} custom-call(f32[72,128]{1,0:T(8,128)} %get-tuple-element.60.coef_ref, f32[6,384,128]{2,1,0:T(8,128)} %copy-done.5, f32[6,384,128]{2,1,0:T(8,128)} %copy-done.10, f32[3,384,128]{2,1,0:T(8,128)} %pad_maximum_fusion.7.row_ref), custom_call_target="tpu_custom_call" | custom-call | flops 10871635968 | bytes 3538944 | tf_op jit(solution)/shard_map/chunk/pallas_call | solution.py:175
  157.2 27.3 %chunk.5.refs_0_ = f32[3,1536,384]{2,1,0:T(8,128)} custom-call(f32[72,128]{1,0:T(8,128)} %get-tuple-element.61.coef_ref, f32[6,384,128]{2,1,0:T(8,128)} %copy-done.4, f32[6,384,128]{2,1,0:T(8,128)} %collective-permute-done.11.vx_ref, f32[3,384,128]{2,1,0:T(8,128)} %pad_maximum_fusion.6.row_ref, ...), custom_call_target="tpu_custom_call", output_to_operand_aliasing={{}: (4, {})} | custom-call | flops 10871635968 | bytes 3538944 | tf_op jit(solution)/shard_map/chunk/pallas_call | solution.py:175
  185.6 27.3 %chunk.6.refs_0_ = f32[3,1536,384]{2,1,0:T(8,128)} custom-call(f32[72,128]{1,0:T(8,128)} %get-tuple-element.62.coef_ref, f32[6,384,128]{2,1,0:T(8,128)} %copy-done.6, f32[6,384,128]{2,1,0:T(8,128)} %copy-done.11, f32[3,384,128]{2,1,0:T(8,128)} %pad_maximum_fusion.5.row_ref, f32[3,1536,384]{2,1,0:T(8,128)} %chunk.5.refs_0_), custom_call_target="tpu_custom_call", output_to_operand_aliasing={{}: (4, {})} | custom-call | flops 10871635968 | bytes 3538944 | tf_op jit(solution)/shard_map/chunk/pallas_call | solution.py:175
  213.9 27.3 %chunk.7 = f32[3,1536,384]{2,1,0:T(8,128)} custom-call(f32[72,128]{1,0:T(8,128)} %get-tuple-element.63.coef_ref, f32[6,384,128]{2,1,0:T(8,128)} %copy-done.7, f32[6,384,128]{2,1,0:T(8,128)} %copy-done.12, f32[3,384,128]{2,1,0:T(8,128)} %pad_maximum_fusion.4.row_ref, f32[3,1536,384]{2,1,0:T(8,128)} %chunk.6.refs_0_), custom_call_target="tpu_custom_call", output_to_operand_aliasing={{}: (4, {})} | custom-call | flops 10871635968 | bytes 3538944 | tf_op jit(solution)/shard_map/chunk/pallas_call | solution.py:175
  241.2 3.5 %fusion.37 = (f32[1,1536,384]{2,1,0:T(8,128)S(1)}, f32[1,1536,384]{2,1,0:T(8,128)S(1)}, f32[1,1536,384]{2,1,0:T(8,128)S(1)}) fusion(f32[3,1536,384]{2,1,0:T(8,128)} %chunk.7), kind=kLoop, calls=%fused_computation.162 | loop fusion | bytes 14155776 | tf_op jit(solution)/shard_map/slice | solution.py:305
  250.9 1.6 collective-permute-start.20
  254.1 1.6 collective-permute-start.26
  257.5 9.7 %collective-permute-done.20 = f32[4,2,48,384]{3,2,0,1:T(8,128)S(1)} collective-permute-done((f32[4,2,48,384]{3,2,0,1:T(8,128)S(1)}, f32[4,2,48,384]{3,2,0,1:T(8,128)S(1)}, u32[]{:S(2)}, u32[]{:S(2)}) %collective-permute-start.20) | collective-permute-done | bytes 589856 | tf_op jit(solution)/shard_map/ppermute | solution.py:242
  267.3 1.6 collective-permute-start.21
  271.9 7.9 %collective-permute-done.32 = f32[4,2,48,384]{3,2,0,1:T(8,128)S(1)} collective-permute-done((f32[4,2,48,384]{3,2,0,1:T(8,128)S(1)}, f32[4,2,48,384]{3,2,0,1:T(8,128)S(1)}, u32[]{:S(2)}, u32[]{:S(2)}) %collective-permute-start.32) | collective-permute-done | bytes 589856 | tf_op jit(solution)/shard_map/ppermute | solution.py:242
  279.9 1.6 collective-permute-start.33
  282.1 5.7 %collective-permute-start.22 = (f32[4,48,96]{2,1,0:T(8,128)S(1)}, f32[4,48,96]{2,1,0:T(8,128)S(1)}, u32[]{:S(2)}, u32[]{:S(2)}) collective-permute-start(f32[4,48,96]{2,1,0:T(8,128)S(1)} %bitcast.116), channel_id=1, source_target_pairs={{0,1},{1,0},{2,3},{3,2},{4,5},{5,4},{6,7},{7,6},{8,9},{9,8},{10,11... | collective-permute-start | bytes 221192 | tf_op jit(solution)/shard_map/ppermute | solution.py:264
  292.0 2.6 collective-permute-start.29
  297.4 7.0 %collective-permute-start.35 = (f32[4,48,96]{2,1,0:T(8,128)S(1)}, f32[4,48,96]{2,1,0:T(8,128)S(1)}, u32[]{:S(2)}, u32[]{:S(2)}) collective-permute-start(f32[4,48,96]{2,1,0:T(8,128)S(1)} %bitcast.114), channel_id=1, source_target_pairs={{0,2},{1,3},{2,0},{3,1},{4,6},{5,7},{6,4},{7,5},{8,10},{9,11},{10,... | collective-permute-start | bytes 221192 | tf_op jit(solution)/shard_map/ppermute | solution.py:264
  305.4 2.4 collective-permute-start.36
  307.8 6.0 %collective-permute-done.35 = f32[4,48,96]{2,1,0:T(8,128)S(1)} collective-permute-done((f32[4,48,96]{2,1,0:T(8,128)S(1)}, f32[4,48,96]{2,1,0:T(8,128)S(1)}, u32[]{:S(2)}, u32[]{:S(2)}) %collective-permute-start.35) | collective-permute-done | bytes 73760 | tf_op jit(solution)/shard_map/ppermute | solution.py:264
  (147 shorter events, 43.4 us)
Async XLA Ops:
  9.2 19.7 %collective-permute-start.16 = (f32[3,96,128]{2,1,0:T(8,128)}, f32[3,96,128]{2,1,0:T(8,128)}, u32[]{:S(2)}, u32[]{:S(2)}) collective-permute-start(f32[3,96,128]{2,1,0:T(8,128)} %pad_maximum_fusion.9), channel_id=1, source_target_pairs={{0,1},{1,0},{2,3},{3,2},{4,5},{5,4},{6,7},{7,6},{8,9},{9,8},{10,11... | collective-permute-start | bytes 442376 | tf_op jit(solution)/shard_map/ppermute | solution.py:288
  13.1 15.9 %collective-permute-start.17 = (f32[3,96,128]{2,1,0:T(8,128)}, f32[3,96,128]{2,1,0:T(8,128)}, u32[]{:S(2)}, u32[]{:S(2)}) collective-permute-start(f32[3,96,128]{2,1,0:T(8,128)} %pad_maximum_fusion.10), channel_id=1, source_target_pairs={{0,2},{1,3},{2,0},{3,1},{4,6},{5,7},{6,4},{7,5},{8,10},{9,11},{10,... | collective-permute-start | bytes 442376 | tf_op jit(solution)/shard_map/ppermute | solution.py:288
  16.4 17.9 %collective-permute-start.18 = (f32[3,96,128]{2,1,0:T(8,128)}, f32[3,96,128]{2,1,0:T(8,128)}, u32[]{:S(2)}, u32[]{:S(2)}) collective-permute-start(f32[3,96,128]{2,1,0:T(8,128)} %pad_maximum_fusion.11), channel_id=1, source_target_pairs={{0,3},{1,2},{2,1},{3,0},{4,7},{5,6},{6,5},{7,4},{8,11},{9,10},{10,... | collective-permute-start | bytes 442376 | tf_op jit(solution)/shard_map/ppermute | solution.py:288
  20.4 14.1 %collective-permute-start.12 = (f32[6,96,128]{2,1,0:T(8,128)}, f32[6,96,128]{2,1,0:T(8,128)}, u32[]{:S(2)}, u32[]{:S(2)}) collective-permute-start(f32[6,96,128]{2,1,0:T(8,128)} %get-tuple-element.23), channel_id=1, source_target_pairs={{0,1},{1,0},{2,3},{3,2},{4,5},{5,4},{6,7},{7,6},{8,9},{9,8},{10,11... | collective-permute-start | bytes 884744 | tf_op jit(solution)/shard_map/ppermute | solution.py:288
  21.3 34.4 %collective-permute-start.13 = (f32[6,96,128]{2,1,0:T(8,128)}, f32[6,96,128]{2,1,0:T(8,128)}, u32[]{:S(2)}, u32[]{:S(2)}) collective-permute-start(f32[6,96,128]{2,1,0:T(8,128)} %get-tuple-element.22), channel_id=1, source_target_pairs={{0,2},{1,3},{2,0},{3,1},{4,6},{5,7},{6,4},{7,5},{8,10},{9,11},{10,... | collective-permute-start | bytes 884744 | tf_op jit(solution)/shard_map/ppermute | solution.py:288
  28.9 27.8 %collective-permute-start.14 = (f32[6,96,128]{2,1,0:T(8,128)}, f32[6,96,128]{2,1,0:T(8,128)S(1)}, u32[]{:S(2)}, u32[]{:S(2)}) collective-permute-start(f32[6,96,128]{2,1,0:T(8,128)} %get-tuple-element.21), channel_id=1, source_target_pairs={{0,3},{1,2},{2,1},{3,0},{4,7},{5,6},{6,5},{7,4},{8,11},{9,10},{10,... | collective-permute-start | bytes 884744 | tf_op jit(solution)/shard_map/ppermute | solution.py:288
  29.0 40.7 %collective-permute-start.10 = (f32[6,96,128]{2,1,0:T(8,128)}, f32[6,96,128]{2,1,0:T(8,128)S(1)}, u32[]{:S(2)}, u32[]{:S(2)}) collective-permute-start(f32[6,96,128]{2,1,0:T(8,128)} %get-tuple-element.24), channel_id=1, source_target_pairs={{0,3},{1,2},{2,1},{3,0},{4,7},{5,6},{6,5},{7,4},{8,11},{9,10},{10,... | collective-permute-start | bytes 884744 | tf_op jit(solution)/shard_map/ppermute | solution.py:288
  34.3 38.8 %collective-permute-start.8 = (f32[6,96,128]{2,1,0:T(8,128)}, f32[6,96,128]{2,1,0:T(8,128)S(1)}, u32[]{:S(2)}, u32[]{:S(2)}) collective-permute-start(f32[6,96,128]{2,1,0:T(8,128)} %get-tuple-element.26), channel_id=1, source_target_pairs={{0,1},{1,0},{2,3},{3,2},{4,5},{5,4},{6,7},{7,6},{8,9},{9,8},{10,11... | collective-permute-start | bytes 884744 | tf_op jit(solution)/shard_map/ppermute | solution.py:288
  34.5 59.1 %collective-permute-start.9 = (f32[6,96,128]{2,1,0:T(8,128)}, f32[6,96,128]{2,1,0:T(8,128)S(1)}, u32[]{:S(2)}, u32[]{:S(2)}) collective-permute-start(f32[6,96,128]{2,1,0:T(8,128)} %get-tuple-element.25), channel_id=1, source_target_pairs={{0,2},{1,3},{2,0},{3,1},{4,6},{5,7},{6,4},{7,5},{8,10},{9,11},{10,... | collective-permute-start | bytes 884744 | tf_op jit(solution)/shard_map/ppermute | solution.py:288
  55.7 37.9 %collective-permute-start.4 = (f32[6,96,128]{2,1,0:T(8,128)}, f32[6,96,128]{2,1,0:T(8,128)S(1)}, u32[]{:S(2)}, u32[]{:S(2)}) collective-permute-start(f32[6,96,128]{2,1,0:T(8,128)} %get-tuple-element.30), channel_id=1, source_target_pairs={{0,1},{1,0},{2,3},{3,2},{4,5},{5,4},{6,7},{7,6},{8,9},{9,8},{10,11... | collective-permute-start | bytes 884744 | tf_op jit(solution)/shard_map/ppermute | solution.py:288
  56.7 55.8 %collective-permute-start.5 = (f32[6,96,128]{2,1,0:T(8,128)}, f32[6,96,128]{2,1,0:T(8,128)S(1)}, u32[]{:S(2)}, u32[]{:S(2)}) collective-permute-start(f32[6,96,128]{2,1,0:T(8,128)} %get-tuple-element.29), channel_id=1, source_target_pairs={{0,2},{1,3},{2,0},{3,1},{4,6},{5,7},{6,4},{7,5},{8,10},{9,11},{10,... | collective-permute-start | bytes 884744 | tf_op jit(solution)/shard_map/ppermute | solution.py:288
  69.7 42.8 %collective-permute-start.6 = (f32[6,96,128]{2,1,0:T(8,128)}, f32[6,96,128]{2,1,0:T(8,128)S(1)}, u32[]{:S(2)}, u32[]{:S(2)}) collective-permute-start(f32[6,96,128]{2,1,0:T(8,128)} %get-tuple-element.28), channel_id=1, source_target_pairs={{0,3},{1,2},{2,1},{3,0},{4,7},{5,6},{6,5},{7,4},{8,11},{9,10},{10,... | collective-permute-start | bytes 884744 | tf_op jit(solution)/shard_map/ppermute | solution.py:288
  73.1 42.0 %collective-permute-start = (f32[6,96,128]{2,1,0:T(8,128)S(1)}, f32[6,96,128]{2,1,0:T(8,128)S(1)}, u32[]{:S(2)}, u32[]{:S(2)}) collective-permute-start(f32[6,96,128]{2,1,0:T(8,128)S(1)} %get-tuple-element.34), channel_id=1, source_target_pairs={{0,1},{1,0},{2,3},{3,2},{4,5},{5,4},{6,7},{7,6},{8,9},{9,8},{10,11... | collective-permute-start | bytes 884744 | tf_op jit(solution)/shard_map/ppermute | solution.py:288
  93.6 31.5 %collective-permute-start.1 = (f32[6,96,128]{2,1,0:T(8,128)S(1)}, f32[6,96,128]{2,1,0:T(8,128)S(1)}, u32[]{:S(2)}, u32[]{:S(2)}) collective-permute-start(f32[6,96,128]{2,1,0:T(8,128)S(1)} %get-tuple-element.33), channel_id=1, source_target_pairs={{0,2},{1,3},{2,0},{3,1},{4,6},{5,7},{6,4},{7,5},{8,10},{9,11},{10,... | collective-permute-start | bytes 884744 | tf_op jit(solution)/shard_map/ppermute | solution.py:288
  93.6 31.5 %collective-permute-start.2 = (f32[6,96,128]{2,1,0:T(8,128)S(1)}, f32[6,96,128]{2,1,0:T(8,128)S(1)}, u32[]{:S(2)}, u32[]{:S(2)}) collective-permute-start(f32[6,96,128]{2,1,0:T(8,128)S(1)} %get-tuple-element.32), channel_id=1, source_target_pairs={{0,3},{1,2},{2,1},{3,0},{4,7},{5,6},{6,5},{7,4},{8,11},{9,10},{10,... | collective-permute-start | bytes 884744 | tf_op jit(solution)/shard_map/ppermute | solution.py:288
  112.5 17.1 %collective-permute-start.15 = (f32[6,384,128]{2,1,0:T(8,128)S(1)}, f32[6,384,128]{2,1,0:T(8,128)S(1)}, u32[]{:S(2)}, u32[]{:S(2)}) collective-permute-start(f32[6,384,128]{2,1,0:T(8,128)S(1)} %pad_maximum_fusion.3.v_ref), channel_id=1, source_target_pairs={{0,28},{4,0},{8,4},{12,8},{16,12},{20,16},{24,20},{28,24},{1,29},{... | collective-permute-start | bytes 3538952 | tf_op jit(solution)/shard_map/ppermute | solution.py:296
  112.5 44.7 %collective-permute-start.11 = (f32[6,384,128]{2,1,0:T(8,128)S(1)}, f32[6,384,128]{2,1,0:T(8,128)}, u32[]{:S(2)}, u32[]{:S(2)}) collective-permute-start(f32[6,384,128]{2,1,0:T(8,128)S(1)} %pad_maximum_fusion.2.v_ref), channel_id=1, source_target_pairs={{0,28},{4,0},{8,4},{12,8},{16,12},{20,16},{24,20},{28,24},{1,29},{... | collective-permute-start | bytes 3538952 | tf_op jit(solution)/shard_map/ppermute | solution.py:296
  115.2 69.4 %collective-permute-start.7 = (f32[6,384,128]{2,1,0:T(8,128)S(1)}, f32[6,384,128]{2,1,0:T(8,128)S(1)}, u32[]{:S(2)}, u32[]{:S(2)}) collective-permute-start(f32[6,384,128]{2,1,0:T(8,128)S(1)} %pad_maximum_fusion.1.v_ref), channel_id=1, source_target_pairs={{0,28},{4,0},{8,4},{12,8},{16,12},{20,16},{24,20},{28,24},{1,29},{... | collective-permute-start | bytes 3538952 | tf_op jit(solution)/shard_map/ppermute | solution.py:296
  125.2 87.7 %collective-permute-start.3 = (f32[6,384,128]{2,1,0:T(8,128)S(1)}, f32[6,384,128]{2,1,0:T(8,128)S(1)}, u32[]{:S(2)}, u32[]{:S(2)}) collective-permute-start(f32[6,384,128]{2,1,0:T(8,128)S(1)} %pad_maximum_fusion.v_ref), channel_id=1, source_target_pairs={{0,28},{4,0},{8,4},{12,8},{16,12},{20,16},{24,20},{28,24},{1,29},{... | collective-permute-start | bytes 3538952 | tf_op jit(solution)/shard_map/ppermute | solution.py:296
  250.9 16.3 %collective-permute-start.20 = (f32[4,2,48,384]{3,2,0,1:T(8,128)S(1)}, f32[4,2,48,384]{3,2,0,1:T(8,128)S(1)}, u32[]{:S(2)}, u32[]{:S(2)}) collective-permute-start(f32[4,2,48,384]{3,2,0,1:T(8,128)S(1)} %bitcast.103), channel_id=1, source_target_pairs={{0,8},{4,12},{8,0},{12,4},{16,24},{20,28},{24,16},{28,20},{1,9},{5... | collective-permute-start | bytes 1769480 | tf_op jit(solution)/shard_map/ppermute | solution.py:242
  254.1 16.3 %collective-permute-start.26 = (f32[4,2,48,384]{3,2,0,1:T(8,128)S(1)}, f32[4,2,48,384]{3,2,0,1:T(8,128)S(1)}, u32[]{:S(2)}, u32[]{:S(2)}) collective-permute-start(f32[4,2,48,384]{3,2,0,1:T(8,128)S(1)} %bitcast.104), channel_id=1, source_target_pairs={{0,16},{4,20},{8,24},{12,28},{16,0},{20,4},{24,8},{28,12},{1,17},{... | collective-permute-start | bytes 1769480 | tf_op jit(solution)/shard_map/ppermute | solution.py:242
  256.0 23.9 %collective-permute-start.32 = (f32[4,2,48,384]{3,2,0,1:T(8,128)S(1)}, f32[4,2,48,384]{3,2,0,1:T(8,128)S(1)}, u32[]{:S(2)}, u32[]{:S(2)}) collective-permute-start(f32[4,2,48,384]{3,2,0,1:T(8,128)S(1)} %bitcast.105), channel_id=1, source_target_pairs={{0,8},{4,12},{8,0},{12,4},{16,24},{20,28},{24,16},{28,20},{1,9},{5... | collective-permute-start | bytes 1769480 | tf_op jit(solution)/shard_map/ppermute | solution.py:242
  267.3 14.2 %collective-permute-start.21 = (f32[4,48,384]{2,1,0:T(8,128)S(1)}, f32[4,48,384]{2,1,0:T(8,128)S(1)}, u32[]{:S(2)}, u32[]{:S(2)}) collective-permute-start(f32[4,48,384]{2,1,0:T(8,128)S(1)} %dynamic-slice_bitcast_fusion.5), channel_id=1, source_target_pairs={{0,16},{4,20},{8,24},{12,28},{16,0},{20,4},{24,8},{28,12},{1,17},{... | collective-permute-start | bytes 884744 | tf_op jit(solution)/shard_map/ppermute | solution.py:242
  270.4 19.9 %collective-permute-start.27 = (f32[4,48,384]{2,1,0:T(8,128)S(1)}, f32[4,48,384]{2,1,0:T(8,128)S(1)}, u32[]{:S(2)}, u32[]{:S(2)}) collective-permute-start(f32[4,48,384]{2,1,0:T(8,128)S(1)} %dynamic-slice_bitcast_fusion.4), channel_id=1, source_target_pairs={{0,8},{4,12},{8,0},{12,4},{16,24},{20,28},{24,16},{28,20},{1,9},{5... | collective-permute-start | bytes 884744 | tf_op jit(solution)/shard_map/ppermute | solution.py:242
  279.9 12.1 %collective-permute-start.33 = (f32[4,48,384]{2,1,0:T(8,128)S(1)}, f32[4,48,384]{2,1,0:T(8,128)S(1)}, u32[]{:S(2)}, u32[]{:S(2)}) collective-permute-start(f32[4,48,384]{2,1,0:T(8,128)S(1)} %dynamic-slice_bitcast_fusion.3), channel_id=1, source_target_pairs={{0,16},{4,20},{8,24},{12,28},{16,0},{20,4},{24,8},{28,12},{1,17},{... | collective-permute-start | bytes 884744 | tf_op jit(solution)/shard_map/ppermute | solution.py:242
  282.1 13.1 %collective-permute-start.22 = (f32[4,48,96]{2,1,0:T(8,128)S(1)}, f32[4,48,96]{2,1,0:T(8,128)S(1)}, u32[]{:S(2)}, u32[]{:S(2)}) collective-permute-start(f32[4,48,96]{2,1,0:T(8,128)S(1)} %bitcast.116), channel_id=1, source_target_pairs={{0,1},{1,0},{2,3},{3,2},{4,5},{5,4},{6,7},{7,6},{8,9},{9,8},{10,11... | collective-permute-start | bytes 221192 | tf_op jit(solution)/shard_map/ppermute | solution.py:264
  287.8 9.6 %collective-permute-start.23 = (f32[4,48,96]{2,1,0:T(8,128)S(1)}, f32[4,48,96]{2,1,0:T(8,128)S(1)}, u32[]{:S(2)}, u32[]{:S(2)}) collective-permute-start(f32[4,48,96]{2,1,0:T(8,128)S(1)} %bitcast.112), channel_id=1, source_target_pairs={{0,2},{1,3},{2,0},{3,1},{4,6},{5,7},{6,4},{7,5},{8,10},{9,11},{10,... | collective-permute-start | bytes 221192 | tf_op jit(solution)/shard_map/ppermute | solution.py:264
  290.9 14.5 %collective-permute-start.28 = (f32[4,48,96]{2,1,0:T(8,128)S(1)}, f32[4,48,96]{2,1,0:T(8,128)S(1)}, u32[]{:S(2)}, u32[]{:S(2)}) collective-permute-start(f32[4,48,96]{2,1,0:T(8,128)S(1)} %bitcast.115), channel_id=1, source_target_pairs={{0,1},{1,0},{2,3},{3,2},{4,5},{5,4},{6,7},{7,6},{8,9},{9,8},{10,11... | collective-permute-start | bytes 221192 | tf_op jit(solution)/shard_map/ppermute | solution.py:264
  292.0 15.8 %collective-permute-start.29 = (f32[4,48,96]{2,1,0:T(8,128)S(1)}, f32[4,48,96]{2,1,0:T(8,128)S(1)}, u32[]{:S(2)}, u32[]{:S(2)}) collective-permute-start(f32[4,48,96]{2,1,0:T(8,128)S(1)} %bitcast.111), channel_id=1, source_target_pairs={{0,2},{1,3},{2,0},{3,1},{4,6},{5,7},{6,4},{7,5},{8,10},{9,11},{10,... | collective-permute-start | bytes 221192 | tf_op jit(solution)/shard_map/ppermute | solution.py:264
  295.2 12.6 %collective-permute-start.30 = (f32[4,48,96]{2,1,0:T(8,128)S(1)}, f32[4,48,96]{2,1,0:T(8,128)S(1)}, u32[]{:S(2)}, u32[]{:S(2)}) collective-permute-start(f32[4,48,96]{2,1,0:T(8,128)S(1)} %bitcast.110), channel_id=1, source_target_pairs={{0,3},{1,2},{2,1},{3,0},{4,7},{5,6},{6,5},{7,4},{8,11},{9,10},{10,... | collective-permute-start | bytes 221192 | tf_op jit(solution)/shard_map/ppermute | solution.py:264
  297.4 10.4 %collective-permute-start.34 = (f32[4,48,96]{2,1,0:T(8,128)S(1)}, f32[4,48,96]{2,1,0:T(8,128)S(1)}, u32[]{:S(2)}, u32[]{:S(2)}) collective-permute-start(f32[4,48,96]{2,1,0:T(8,128)S(1)} %bitcast.117), channel_id=1, source_target_pairs={{0,1},{1,0},{2,3},{3,2},{4,5},{5,4},{6,7},{7,6},{8,9},{9,8},{10,11... | collective-permute-start | bytes 221192 | tf_op jit(solution)/shard_map/ppermute | solution.py:264
  297.4 16.3 %collective-permute-start.35 = (f32[4,48,96]{2,1,0:T(8,128)S(1)}, f32[4,48,96]{2,1,0:T(8,128)S(1)}, u32[]{:S(2)}, u32[]{:S(2)}) collective-permute-start(f32[4,48,96]{2,1,0:T(8,128)S(1)} %bitcast.114), channel_id=1, source_target_pairs={{0,2},{1,3},{2,0},{3,1},{4,6},{5,7},{6,4},{7,5},{8,10},{9,11},{10,... | collective-permute-start | bytes 221192 | tf_op jit(solution)/shard_map/ppermute | solution.py:264
  (19 other events, 136.5 us)

commit v2 on v1

v2 whole, which is shorter than its diff:
```python
import functools

import jax
import jax.numpy as jnp
from jax import lax
from jax.experimental import pallas as pl
from jax.experimental.pallas import tpu as pltpu
from jax.sharding import PartitionSpec as P


LANES = 128
PLANE_Z = 64
TILE = 16
COLS = 256
F32 = jnp.float32
BF16 = jnp.bfloat16


def xor_pairs(size, k):
    return [(i, i ^ k) for i in range(size)]


def bits_of(size):
    return size.bit_length() - 1


def split(value):
    high = value.astype(BF16)
    return high, (value - high.astype(F32)).astype(BF16)


def matvec(link, re, im, dagger):
    out_re, out_im = [], []
    for row in range(3):
        acc_re = acc_im = None
        for col in range(3):
            u_re, u_im = link[col * 3 + row] if dagger else link[row * 3 + col]
            if dagger:
                t_re = u_re * re[col] + u_im * im[col]
                t_im = u_re * im[col] - u_im * re[col]
            else:
                t_re = u_re * re[col] - u_im * im[col]
                t_im = u_re * im[col] + u_im * re[col]
            acc_re = t_re if acc_re is None else acc_re + t_re
            acc_im = t_im if acc_im is None else acc_im + t_im
        out_re.append(acc_re)
        out_im.append(acc_im)
    return out_re, out_im


def tools_of(coef_ref):
    def coef(index):
        return jnp.broadcast_to(coef_ref[pl.ds(index, 1), :], (TILE, LANES))

    def link_of(mu):
        return [(coef(mu * 18 + e), coef(mu * 18 + 9 + e)) for e in range(9)]

    def phased(ref, nv, start, re, im, base):
        for m in range(2):
            cos, sin = coef(base + 2 * m), coef(base + 2 * m + 1)
            rows = pl.ds(pl.multiple_of(m * nv + start, TILE), TILE)
            for c in range(3):
                put(ref, rows, c, re[c] * cos - im[c] * sin)
                put(ref, rows, 3 + c, re[c] * sin + im[c] * cos)

    return coef, link_of, phased


def put(ref, rows, col, value):
    high, rest = split(value)
    ref[0, rows, pl.ds(col * LANES, LANES)] = high
    ref[1, rows, pl.ds(col * LANES, LANES)] = rest


def put_right(ref, nv, start, re, im):
    real = pl.ds(pl.multiple_of(start, TILE), TILE)
    imag = pl.ds(pl.multiple_of(nv + start, TILE), TILE)
    for c in range(3):
        r, i = split(re[c]), split(im[c])
        low, high = pl.ds(c * LANES, LANES), pl.ds((3 + c) * LANES, LANES)
        for half in range(2):
            ref[half, real, low] = r[half]
            ref[half, real, high] = i[half]
            ref[half, imag, low] = i[half]
            ref[half, imag, high] = -r[half]


def collect(block_refs, held, sems):
    copies = []
    for k, ref in enumerate(block_refs):
        own = ref.shape[1]
        to = held.at[:, pl.ds(k * own, own), :]
        copies.append(pltpu.make_async_copy(ref, to, sems.at[k]))
        copies[-1].start()
    return copies


def product(left, right, rows):
    dims = (((1,), (1,)), ((), ()))
    total = None
    for i, j in ((0, 0), (0, 1), (1, 0)):
        term = lax.dot_general(
            left[i], right[j, rows, :], dims, preferred_element_type=F32
        )
        total = term if total is None else total + term
    return total


def finish(mine_ref, total, cols, keep_ref, send_ref):
    count, shard = keep_ref.shape[:2]
    parts = total.reshape(count, 2, shard, total.shape[1])
    first, second = parts[:, 0], parts[:, 1]
    flip = mine_ref[0] == 1
    keep_ref[:, :, cols] = jnp.where(flip, second, first)
    send_ref[:, :, cols] = jnp.where(flip, first, second)


def tiles(nv, tile_of, prepare=None):
    steps = 2 * nv // COLS
    share = nv // steps

    def body(step, carry):
        if prepare is not None:
            for i in range(share // TILE):
                prepare(pl.multiple_of(step * share + i * TILE, TILE))
        tile_of(pl.ds(pl.multiple_of(step * COLS, COLS), COLS))
        return carry

    lax.fori_loop(0, steps, body, 0)


def plane_kernel(n_vec, has_acc, last, packed, nv, mine_ref, coef_ref, *refs):
    refs = list(refs)
    blocks = [refs.pop(0) for _ in range(n_vec)]
    row_blocks = [refs.pop(0) for _ in range(n_vec)]
    acc_ref = refs.pop(0) if has_acc else None
    outs = [refs.pop(0) for _ in range(4 if last else 1)]
    held, held_row, left_v, left_r, right_1, right_2, right_r, sems, row_sems = refs
    coef, link_of, phased = tools_of(coef_ref)
    lane = lax.broadcasted_iota(jnp.int32, (TILE, LANES), 1)
    low = lane < PLANE_Z
    at_end = lane % PLANE_Z == PLANE_Z - 1
    at_start = lane % PLANE_Z == 0
    turn = lambda x, by: pltpu.roll(x, by, 1)

    def load(start):
        rows = pl.ds(start, TILE)
        return [held[c, rows, :] for c in range(3)], [held[3 + c, rows, :] for c in range(3)]

    def prepare_1(start):
        rows = pl.ds(start, TILE)
        re, im = load(start)
        phased(left_v, nv, start, re, im, 54)
        if packed:
            both = [held_row[c, rows, :] for c in range(3)]
            turned = [turn(x, PLANE_Z) for x in both]
            n_re = [jnp.where(low, both[c], turned[c]) for c in range(3)]
            n_im = [jnp.where(low, turned[c], both[c]) for c in range(3)]
        else:
            n_re = [held_row[c, rows, :] for c in range(3)]
            n_im = [held_row[3 + c, rows, :] for c in range(3)]
            n_re = [jnp.where(low, x, turn(x, PLANE_Z)) for x in n_re]
            n_im = [jnp.where(low, x, turn(x, PLANE_Z)) for x in n_im]
        link1 = link_of(1)
        fre = [jnp.where(low, turn(re[c], PLANE_Z), n_re[c]) for c in range(3)]
        fim = [jnp.where(low, turn(im[c], PLANE_Z), n_im[c]) for c in range(3)]
        fre, fim = matvec(link1, fre, fim, False)
        bre, bim = matvec(link1, re, im, True)
        r_re = [turn(x, PLANE_Z) for x in bre]
        r_im = [turn(x, PLANE_Z) for x in bim]
        put_right(
            right_1,
            nv,
            start,
            [jnp.where(low, fre[c], fre[c] - r_re[c]) for c in range(3)],
            [jnp.where(low, fim[c], fim[c] - r_im[c]) for c in range(3)],
        )
        imag = pl.ds(pl.multiple_of(nv + start, TILE), TILE)
        for c in range(3):
            put(right_r, rows, c, -jnp.where(low, r_re[c], bim[c]))
            put(right_r, imag, c, jnp.where(low, -r_im[c], bre[c]))
        for m in range(2):
            a, b = coef(62 + 2 * m), coef(63 + 2 * m)
            to = pl.ds(pl.multiple_of(m * nv + start, TILE), TILE)
            for c in range(3):
                put(left_r, to, c, n_re[c] * a + n_im[c] * b)

    def prepare_2(start):
        re, im = load(start)
        link2 = link_of(2)
        ahead = lambda x: jnp.where(at_end, turn(x, PLANE_Z - 1), turn(x, LANES - 1))
        back = lambda x: jnp.where(at_start, turn(x, PLANE_Z + 1), turn(x, 1))
        zre, zim = matvec(link2, [ahead(x) for x in re], [ahead(x) for x in im], False)
        bre, bim = matvec(link2, re, im, True)
        put_right(
            right_2,
            nv,
            start,
            [zre[c] - back(bre[c]) for c in range(3)],
            [zim[c] - back(bim[c]) for c in range(3)],
        )

    def store(total, cols, pair):
        if has_acc:
            total = total + acc_ref[0, :, cols]
        if last:
            finish(mine_ref, total, cols, *pair)
        else:
            outs[0][0, :, cols] = total

    @pl.when(pl.program_id(0) == 0)
    def _():
        copies = collect(blocks, held, sems) + collect(row_blocks, held_row, row_sems)
        for copy in copies:
            copy.wait()

        def body(step, carry):
            prepare_1(pl.multiple_of(step * TILE, TILE))
            return carry

        lax.fori_loop(0, nv // TILE, body, 0)
        tiles(
            nv,
            lambda cols: store(
                product(left_v, right_1, cols) + product(left_r, right_r, cols), cols, outs[:2]
            ),
            prepare_2,
        )

    @pl.when(pl.program_id(0) == 1)
    def _():
        tiles(nv, lambda cols: store(product(left_v, right_2, cols), cols, outs[2:]))


def cross_kernel(n_vec, has_acc, last, nv, mine_ref, coef_ref, *refs):
    refs = list(refs)
    blocks = [refs.pop(0) for _ in range(n_vec)]
    next_blocks = [refs.pop(0) for _ in range(n_vec)]
    acc_ref = refs.pop(0) if has_acc else None
    outs = [refs.pop(0) for _ in range(2 if last else 1)]
    held, held_next, left_v, left_w, right_w, right_v, forward, sems, next_sems = refs
    _, link_of, phased = tools_of(coef_ref)

    def load(ref, start):
        rows = pl.ds(start, TILE)
        return [ref[c, rows, :] for c in range(3)], [ref[3 + c, rows, :] for c in range(3)]

    def prepare_1(start):
        re, im = load(held, start)
        phased(left_v, nv, start, re, im, 54)
        re, im = load(held_next, start)
        re, im = matvec(link_of(0), re, im, False)
        put_right(right_w, nv, start, re, im)
        rows = pl.ds(start, TILE)
        for c in range(3):
            held_next[c, rows, :] = re[c]
            held_next[3 + c, rows, :] = im[c]

    def prepare_2(start):
        re, im = load(held_next, start)
        phased(left_w, nv, start, re, im, 58)
        re, im = load(held, start)
        put_right(right_v, nv, start, re, im)

    @pl.when(pl.program_id(0) == 0)
    def _():
        copies = collect(blocks, held, sems) + collect(next_blocks, held_next, next_sems)
        for copy in copies:
            copy.wait()

        def body(step, carry):
            prepare_1(pl.multiple_of(step * TILE, TILE))
            return carry

        lax.fori_loop(0, nv // TILE, body, 0)

        def tile_of(cols):
            forward[:, cols] = product(left_v, right_w, cols)

        tiles(nv, tile_of, prepare_2)

        def tile_of(cols):
            total = forward[:, cols] + product(left_w, right_v, cols)
            if has_acc:
                total = total + acc_ref[:, cols]
            if last:
                finish(mine_ref, total, cols, outs[0], outs[1])
            else:
                outs[0][:, cols] = total

        tiles(nv, tile_of)


def chunk_call(kind, mine, coef, blocks, others, acc, last, shard, packed=False):
    n_vec = len(blocks)
    nv = n_vec * blocks[0].shape[1]
    has_acc = acc is not None
    dirs = 2 if kind == "plane" else 1
    whole = lambda shape: pl.BlockSpec(shape, lambda i: (0,) * len(shape))
    if dirs == 2:
        shape = (2, 2 * nv, 2 * nv)
        tile = pl.BlockSpec((1, 2 * nv, 2 * nv), lambda i: (i, 0, 0))
        body = functools.partial(plane_kernel, n_vec, has_acc, last, packed, nv)
    else:
        shape = (2 * nv, 2 * nv)
        tile = pl.BlockSpec(shape, lambda i: (0, 0))
        body = functools.partial(cross_kernel, n_vec, has_acc, last, nv)
    args = [mine, coef] + blocks + others + ([acc] if has_acc else [])
    specs = [pl.BlockSpec(memory_space=pltpu.SMEM), whole(coef.shape)]
    specs += [pl.BlockSpec(memory_space=pl.ANY)] * (2 * n_vec)
    specs += [tile] if has_acc else []
    if last:
        half = (nv // shard, shard, 2 * nv)
        out_shape = [jax.ShapeDtypeStruct(half, F32)] * (2 * dirs)
        out_specs = [whole(half)] * (2 * dirs)
    else:
        out_shape = [jax.ShapeDtypeStruct(shape, F32)]
        out_specs = [tile]
    wide = 6 * LANES
    row_parts = 3 if packed else 6
    if dirs == 2:
        scratch = [
            pltpu.VMEM((6, nv, LANES), F32),
            pltpu.VMEM((row_parts, nv, LANES), F32),
            pltpu.VMEM((2, 2 * nv, wide), BF16),
            pltpu.VMEM((2, 2 * nv, wide // 2), BF16),
            pltpu.VMEM((2, 2 * nv, wide), BF16),
            pltpu.VMEM((2, 2 * nv, wide), BF16),
            pltpu.VMEM((2, 2 * nv, wide // 2), BF16),
        ]
    else:
        scratch = [pltpu.VMEM((6, nv, LANES), F32)] * 2
        scratch += [pltpu.VMEM((2, 2 * nv, wide), BF16)] * 4
        scratch += [pltpu.VMEM((2 * nv, 2 * nv), F32)]
    scratch += [pltpu.SemaphoreType.DMA((n_vec,))] * 2
    flops = 3 * 2 * 4 * nv * nv * wide * 2
    return pl.pallas_call(
        body,
        out_shape=out_shape,
        grid=(dirs,),
        in_specs=specs,
        out_specs=out_specs,
        scratch_shapes=scratch,
        input_output_aliases={2 + 2 * n_vec: 0} if has_acc and not last else {},
        cost_estimate=pl.CostEstimate(
            flops=flops, bytes_accessed=24 * nv * nv, transcendentals=0
        ),
        compiler_params=pltpu.CompilerParams(vmem_limit_bytes=32 * 1024 * 1024),
    )(*args)


def cut_kernel(count, index_ref, *refs):
    for x_ref, o_ref in zip(refs[:count], refs[count:]):
        o_ref[...] = x_ref[...]


def cut(vectors, index):
    count = index.shape[0]
    block = vectors.shape[:4] + (LANES,)
    piece = jax.ShapeDtypeStruct(block, F32)
    outs = pl.pallas_call(
        functools.partial(cut_kernel, count),
        out_shape=[piece] * count,
        grid_spec=pltpu.PrefetchScalarGridSpec(
            num_scalar_prefetch=1,
            grid=(1,),
            in_specs=[
                pl.BlockSpec(block, lambda i, at, k=k: (0, 0, 0, 0, at[k]))
                for k in range(count)
            ],
            out_specs=[pl.BlockSpec(block, lambda i, at: (0,) * 5)] * count,
        ),
        compiler_params=pltpu.CompilerParams(vmem_limit_bytes=32 * 1024 * 1024),
        name="cut",
    )(index, *([vectors] * count))
    return [o.reshape(6, block[2], LANES) for o in outs]


def phase_rows(momenta, xcoord, sites, extent_x, plane_y):
    ycoord = sites // PLANE_Z
    zcoord = sites % PLANE_Z
    p0, p1, p2 = (momenta[:, i][:, None] for i in range(3))
    frac = (p0 * xcoord % extent_x).astype(F32) / extent_x
    frac = frac + (p1 * ycoord[None] % plane_y).astype(F32) / plane_y
    frac = frac + (p2 * zcoord[None] % PLANE_Z).astype(F32) / PLANE_Z
    theta = 2.0 * jnp.pi * frac
    return jnp.cos(theta), jnp.sin(theta)


def coefficients(links, momenta, xcoord, start, subs, extent_x, plane):
    plane_y = plane // PLANE_Z
    width = subs * LANES
    rows = lax.dynamic_slice_in_dim(links.reshape(54, plane), start, width, 1)
    sites = start + jnp.arange(width, dtype=jnp.int32)
    cos, sin = phase_rows(momenta, xcoord, sites, extent_x, plane_y)
    cos_x, sin_x = phase_rows(momenta, xcoord + 1, sites, extent_x, plane_y)
    after = jnp.arange(subs, dtype=jnp.int32)[:, None] * LANES + LANES
    after = start + after + jnp.arange(LANES, dtype=jnp.int32)[None] % PLANE_Z
    cos_r, sin_r = phase_rows(
        momenta, xcoord, after.reshape(-1) % plane, extent_x, plane_y
    )
    low = jnp.arange(width) % LANES < PLANE_Z
    parts = [rows]
    for m in range(2):
        parts += [cos[m : m + 1], sin[m : m + 1]]
    for m in range(2):
        parts += [-cos_x[m : m + 1], -sin_x[m : m + 1]]
    for m in range(2):
        c, s = cos_r[m : m + 1], sin_r[m : m + 1]
        parts += [
            jnp.where(low, c, s),
            jnp.where(low, -s, c),
        ]
    parts.append(jnp.zeros((6, width), F32))
    table = jnp.concatenate(parts, 0)
    return [table[:, i * LANES : (i + 1) * LANES] for i in range(subs)]


def scatter_step(value, axis_dim, mine, axis, bit, size):
    keep = lax.dynamic_index_in_dim(value, mine, axis_dim, keepdims=False)
    send = lax.dynamic_index_in_dim(value, 1 - mine, axis_dim, keepdims=False)
    return keep + lax.ppermute(send, axis, xor_pairs(size, bit))


def reduce_block(keep, send, order, n_space, n_vec):
    s = lax.axis_index("space")
    t = lax.axis_index("vec")
    s_bits, v_bits = bits_of(n_space), bits_of(n_vec)
    lead, nv = (2,), keep.shape[-1] // 2
    value = keep + lax.ppermute(send, "space", xor_pairs(n_space, 1))
    left = list(range(s_bits - 1))
    value = value.reshape(lead + (2,) * len(left) + (nv // n_space, 2 * nv))
    for level in order:
        mine = (s >> (s_bits - 1 - level)) & 1
        if level < v_bits:
            mine = mine ^ ((t >> (v_bits - 1 - level)) & 1)
        value = scatter_step(
            value, len(lead) + left.index(level), mine, "space", 1 << (s_bits - 1 - level), n_space
        )
        left.remove(level)
    for level in range(v_bits):
        value = value.reshape(lead + (nv // n_space, 2, -1, 2, nv // n_vec))
        sent = lax.ppermute(value[..., 1, :], "vec", xor_pairs(n_vec, 1 << level))
        value = value[..., 0, :] + sent
    return value.reshape(lead + (nv // n_space, 2, nv // n_vec))


def on_device(vectors, links, momenta, directions):
    n_space, n_vec = lax.axis_size("space"), lax.axis_size("vec")
    s, t = lax.axis_index("space"), lax.axis_index("vec")
    own = vectors.shape[2]
    plane = vectors.shape[4]
    chunk = plane // n_vec
    subs = chunk // LANES
    nv = own * n_vec
    shard = nv // n_space
    down = [(i, (i - 1) % n_space) for i in range(n_space)]
    to_all = lambda part: [
        lax.ppermute(part[k], "vec", xor_pairs(n_vec, k)) for k in range(1, n_vec)
    ]
    order = list(reversed(range(subs)))
    partner = t ^ jnp.arange(n_vec, dtype=jnp.int32)
    first = jnp.concatenate([partner * subs + order[0], (partner + 1) % n_vec * subs])
    pieces = {}
    cuts = cut(vectors, first)
    pieces[order[0]], rows = cuts[:n_vec], cuts[n_vec:]
    rows = [
        jnp.concatenate([r[:3, :, :PLANE_Z], r[3:, :, :PLANE_Z]], 2) for r in rows
    ]
    got = {order[0]: to_all(pieces[order[0]])}
    rows = [rows[0]] + to_all(rows)
    rest = jnp.concatenate([partner * subs + sub for sub in order[1:]])
    cuts = cut(vectors, rest)
    for step, sub in enumerate(order[1:], 1):
        pieces[sub] = cuts[(step - 1) * n_vec : step * n_vec]
        got[sub] = to_all(pieces[sub])
    tables = coefficients(links, momenta, s, t * chunk, subs, n_space * vectors.shape[3], plane)
    mine = (s & 1).reshape(1).astype(jnp.int32)
    plane_acc = cross_acc = None
    for step, sub in enumerate(order):
        last = step == subs - 1
        blocks = [pieces[sub][0]] + got[sub]
        ahead = [lax.ppermute(x, "space", down) for x in blocks]
        planes = chunk_call(
            "plane", mine, tables[sub], blocks, rows, plane_acc, last, shard, step == 0
        )
        crosses = chunk_call(
            "cross", mine, tables[sub], blocks, ahead, cross_acc, last, shard
        )
        plane_acc, cross_acc = planes[0], crosses[0]
        rows = blocks
    forward = list(reversed(range(bits_of(n_space) - 1)))
    backward = forward[::-1]
    out = [
        reduce_block(*crosses, forward, n_space, n_vec),
        reduce_block(*planes[:2], forward, n_space, n_vec),
        reduce_block(*planes[2:], backward, n_space, n_vec),
    ]
    out = jnp.transpose(jnp.stack(out, 0), (0, 1, 3, 2, 4))
    out = [lax.dynamic_index_in_dim(out, directions[k], 0, keepdims=False) for k in range(3)]
    return jnp.stack(out, 1)


def solution(mesh):
    placed = (
        P(None, None, "vec", "space", None),
        P(None, None, None, None, "space", None),
        P(),
        P(),
    )
    return jax.shard_map(
        on_device,
        mesh=mesh,
        in_specs=placed,
        out_specs=P(None, None, None, "space", "vec"),
        check_vma=False,
    )
```

time: 316 us -> 263 us (0.83)
  waiting for transfers between devices: 75.5 us -> 53.9 us
  Pallas kernels: 109 us -> 94.6 us
  local copies, waits for them, and re-layouts: 29.9 us -> 16.2 us
  starting transfers between devices: 85.1 us -> 75.3 us
  between operations: 0.53 us -> 6.34 us
    ppermute x28 -> x40, waiting for transfers between devices: 55.3 us -> 35.3 us  [the longest x15 21.2 us: on_device(): lax.ppermute(part[k], 'vec', xor_pairs(n_vec, k))]
    pallas_call x4 -> x10, Pallas kernels: 109 us -> 94.6 us  [the longest x8 89.1 us: chunk_call(): pl.pallas_call(body, out_shape=out_shape, grid=(dirs,), in_specs=specs, o...]
    ppermute x28 -> x40, starting transfers between devices: 75.2 us -> 68.6 us  [the longest x15 46 us: on_device(): lax.ppermute(part[k], 'vec', xor_pairs(n_vec, k))]
    concatenate x11 -> x6, other arithmetic: 8.79 us -> 2.58 us  [the longest x4 2.43 us: on_device(): jnp.concatenate([r[:3, :, :PLANE_Z], r[3:, :, :PLANE_Z]], 2)]
    unnamed x29 -> x28, local copies, waits for them, and re-layouts: 11.8 us -> 6.6 us
    add x0 -> x5, other arithmetic: none -> 4.82 us  [the longest x3 4.23 us: reduce_block(): value = keep + lax.ppermute(send, 'space', xor_pairs(n_space, 1))]
    dynamic_slice x7 -> x0, local copies, waits for them, and re-layouts: 4.36 us -> none  [the longest x1 3.98 us: piece(): return lax.dynamic_slice_in_dim(field, start, LANES, 2)]
    slice x8 -> x9, local copies, waits for them, and re-layouts: 6.33 us -> 2.52 us  [the longest x4 0.79 us: on_device(): r[:3, :, :PLANE_Z]]
  transfers between devices with their start and end apart: 37 -> 46, of which waited for: 11 -> 12; matrix products, arithmetic and copies ran while one was open for 8% -> 9% of each run, Pallas kernels for 26% -> 35%
where the time goes in v2:
time: 263 us
  Pallas kernels  94.6 us (36%)
  starting transfers between devices  75.3 us (29%)
  waiting for transfers between devices  53.9 us (20%)
  other arithmetic  16.2 us (6%)
  local copies, waits for them, and re-layouts  16.2 us (6%)
  between operations  6.34 us (2%)
    pallas_call x8, Pallas kernels, chunk_call(): pl.pallas_call(body, out_shape=out_shape, grid=(dirs,), in_specs=specs, o...  89.1 us
    ppermute x15, starting transfers between devices, on_device(): lax.ppermute(part[k], 'vec', xor_pairs(n_vec, k))  46 us
    ppermute x15, waiting for transfers between devices, on_device(): lax.ppermute(part[k], 'vec', xor_pairs(n_vec, k))  21.2 us
    ppermute x6, waiting for transfers between devices, scatter_step(): return keep + lax.ppermute(send, axis, xor_pairs(size, bit))  18.6 us
    ppermute x16, starting transfers between devices, on_device(): ahead = [lax.ppermute(x, 'space', down) for x in blocks]  14.2 us
    ppermute x6, waiting for transfers between devices, reduce_block(): sent = lax.ppermute(value[..., 1, :], 'vec', xor_pairs(n_vec, 1 << level))  13.7 us
    ppermute x6, starting transfers between devices, reduce_block(): sent = lax.ppermute(value[..., 1, :], 'vec', xor_pairs(n_vec, 1 << level))  7.74 us
    ppermute x6, starting transfers between devices, scatter_step(): return keep + lax.ppermute(send, axis, xor_pairs(size, bit))  6.73 us
  transfers between devices with their start and end apart: 46, of which 12 were waited for; matrix products, arithmetic and copies ran while one was open for 9% of the time, Pallas kernels for 35%

profile of v2, /device:TPU:0, one launch (start us, length us, event | category | flops | bytes accessed | tf_op | source)
XLA Modules:
  0.0 262.6 jit_solution(11624438389196497121)
XLA Ops:
  1.2 2.3 copy-done
  3.5 2.3 cut.3
  5.9 3.1 %collective-permute-start.21 = (f32[6,96,128]{2,1,0:T(8,128)S(1)}, f32[6,96,128]{2,1,0:T(8,128)S(1)}, u32[]{:S(2)}, u32[]{:S(2)}) collective-permute-start(f32[6,96,128]{2,1,0:T(8,128)S(1)} %bitcast.154), channel_id=1, source_target_pairs={{0,1},{1,0},{2,3},{3,2},{4,5},{5,4},{6,7},{7,6},{8,9},{9,8},{10,11... | collective-permute-start | bytes 884744 | tf_op jit(solution)/shard_map/ppermute | solution.py:459
  9.0 2.6 collective-permute-start.22
  14.1 3.5 %collective-permute-start.34 = (f32[3,96,128]{2,1,0:T(8,128)}, f32[3,96,128]{2,1,0:T(8,128)}, u32[]{:S(2)}, u32[]{:S(2)}) collective-permute-start(f32[3,96,128]{2,1,0:T(8,128)} %pad_maximum_fusion.4), channel_id=1, source_target_pairs={{0,2},{1,3},{2,0},{3,1},{4,6},{5,7},{6,4},{7,5},{8,10},{9,11},{10,... | collective-permute-start | bytes 442376 | tf_op jit(solution)/shard_map/ppermute | solution.py:459
  24.5 7.9 %collective-permute-done.33.refs_5_ = f32[3,96,128]{2,1,0:T(8,128)S(1)} collective-permute-done((f32[3,96,128]{2,1,0:T(8,128)}, f32[3,96,128]{2,1,0:T(8,128)S(1)}, u32[]{:S(2)}, u32[]{:S(2)}) %collective-permute-start.33) | collective-permute-done | bytes 147488 | tf_op jit(solution)/shard_map/ppermute | solution.py:459
  32.4 3.2 %collective-permute-start.35 = (f32[3,96,128]{2,1,0:T(8,128)}, f32[3,96,128]{2,1,0:T(8,128)S(1)}, u32[]{:S(2)}, u32[]{:S(2)}) collective-permute-start(f32[3,96,128]{2,1,0:T(8,128)} %pad_maximum_fusion.5), channel_id=1, source_target_pairs={{0,3},{1,2},{2,1},{3,0},{4,7},{5,6},{6,5},{7,4},{8,11},{9,10},{10,... | collective-permute-start | bytes 442376 | tf_op jit(solution)/shard_map/ppermute | solution.py:459
  35.6 2.3 copy-done.1
  38.0 3.2 %cut.2 = (f32[2,3,96,1,128]{4,3,2,1,0:T(1,128)S(1)}, f32[2,3,96,1,128]{4,3,2,1,0:T(1,128)S(1)}, f32[2,3,96,1,128]{4,3,2,1,0:T(1,128)S(1)}, f32[2,3,96,1,128]{4,3...) custom-call(s32[12]{0:T(128)S(1)} %pad_add_fusion.index_ref, ...), custom_call_target="tpu_custom_call" | custom-call | tf_op jit(solution)/shard_map/cut/pallas_call | solution.py:361
  41.3 7.0 %collective-permute-done.34.refs_6_ = f32[3,96,128]{2,1,0:T(8,128)} collective-permute-done((f32[3,96,128]{2,1,0:T(8,128)}, f32[3,96,128]{2,1,0:T(8,128)}, u32[]{:S(2)}, u32[]{:S(2)}) %collective-permute-start.34) | collective-permute-done | bytes 147488 | tf_op jit(solution)/shard_map/ppermute | solution.py:459
  53.4 13.1 %shard_map.50.refs_8_ = f32[2,768,768]{2,1,0:T(8,128)S(1)} custom-call(s32[1]{0:T(128)} %bitcast.mine_ref, f32[72,128]{1,0:T(8,128)S(1)} %get-tuple-element.80.coef_ref, f32[6,96,128]{2,1,0:T(8,128)S(1)} %bitcast.142, f32[6,96,128]{2,1,0:T(8,128)S(1)} %collective-permute-done.21.refs_1_.refs_5_, f32[6,96,128]{2,1,0:T(8,128)S(1)} %collective-permute-done.22.refs_2_.refs_6_, ...), custom_call_target="tpu_custom_call" | custom-call | flops 5435817984 | bytes 3538944 | tf_op jit(solution)/shard_map/pallas_call | solution.py:337
  66.5 3.0 %collective-permute-done.14.refs_1_.refs_5_ = f32[6,96,128]{2,1,0:T(8,128)S(1)} collective-permute-done((f32[6,96,128]{2,1,0:T(8,128)S(1)}, f32[6,96,128]{2,1,0:T(8,128)S(1)}, u32[]{:S(2)}, u32[]{:S(2)}) %collective-permute-start.14) | collective-permute-done | bytes 294944 | tf_op jit(solution)/shard_map/ppermute | solution.py:459
  69.4 4.9 %collective-permute-start.8 = (f32[6,96,128]{2,1,0:T(8,128)S(1)}, f32[6,96,128]{2,1,0:T(8,128)S(1)}, u32[]{:S(2)}, u32[]{:S(2)}) collective-permute-start(f32[6,96,128]{2,1,0:T(8,128)S(1)} %bitcast.163), channel_id=1, source_target_pairs={{0,2},{1,3},{2,0},{3,1},{4,6},{5,7},{6,4},{7,5},{8,10},{9,11},{10,... | collective-permute-start | bytes 884744 | tf_op jit(solution)/shard_map/ppermute | solution.py:459
  74.3 3.3 %collective-permute-done.16.refs_3_.refs_7_ = f32[6,96,128]{2,1,0:T(8,128)S(1)} collective-permute-done((f32[6,96,128]{2,1,0:T(8,128)S(1)}, f32[6,96,128]{2,1,0:T(8,128)S(1)}, u32[]{:S(2)}, u32[]{:S(2)}) %collective-permute-start.16) | collective-permute-done | bytes 294944 | tf_op jit(solution)/shard_map/ppermute | solution.py:459
  79.0 13.4 %shard_map.51.refs_8_ = f32[2,768,768]{2,1,0:T(8,128)S(1)} custom-call(s32[1]{0:T(128)} %bitcast.mine_ref, f32[72,128]{1,0:T(8,128)S(1)} %get-tuple-element.81.coef_ref, f32[6,96,128]{2,1,0:T(8,128)S(1)} %bitcast.155, f32[6,96,128]{2,1,0:T(8,128)S(1)} %collective-permute-done.14.refs_1_.refs_5_, ...), custom_call_target="tpu_custom_call", output_to_operand_aliasing={{}: (10, {})} | custom-call | flops 5435817984 | bytes 3538944 | tf_op jit(solution)/shard_map/pallas_call | solution.py:337
  92.4 18.8 %collective-permute-start.1 = (f32[6,96,128]{2,1,0:T(8,128)S(1)}, f32[6,96,128]{2,1,0:T(8,128)S(1)}, u32[]{:S(2)}, u32[]{:S(2)}) collective-permute-start(f32[6,96,128]{2,1,0:T(8,128)S(1)} %bitcast.160), channel_id=1, source_target_pairs={{0,2},{1,3},{2,0},{3,1},{4,6},{5,7},{6,4},{7,5},{8,10},{9,11},{10,... | collective-permute-start | bytes 884744 | tf_op jit(solution)/shard_map/ppermute | solution.py:459
  111.2 2.9 %collective-permute-start.2 = (f32[6,96,128]{2,1,0:T(8,128)S(1)}, f32[6,96,128]{2,1,0:T(8,128)S(1)}, u32[]{:S(2)}, u32[]{:S(2)}) collective-permute-start(f32[6,96,128]{2,1,0:T(8,128)S(1)} %bitcast.159), channel_id=1, source_target_pairs={{0,3},{1,2},{2,1},{3,0},{4,7},{5,6},{6,5},{7,4},{8,11},{9,10},{10,... | collective-permute-start | bytes 884744 | tf_op jit(solution)/shard_map/ppermute | solution.py:459
  114.1 12.4 %shard_map.52.refs_8_ = f32[2,768,768]{2,1,0:T(8,128)S(1)} custom-call(s32[1]{0:T(128)} %bitcast.mine_ref, f32[72,128]{1,0:T(8,128)S(1)} %get-tuple-element.82.coef_ref, f32[6,96,128]{2,1,0:T(8,128)S(1)} %bitcast.148, f32[6,96,128]{2,1,0:T(8,128)S(1)} %collective-permute-done.7.refs_1_.refs_5_, ...), custom_call_target="tpu_custom_call", output_to_operand_aliasing={{}: (10, {})} | custom-call | flops 5435817984 | bytes 3538944 | tf_op jit(solution)/shard_map/pallas_call | solution.py:337
  126.6 2.6 collective-permute-start.25
  129.8 13.7 %shard_map.53 = (f32[8,48,768]{2,1,0:T(8,128)S(1)}, f32[8,48,768]{2,1,0:T(8,128)}, f32[8,48,768]{2,1,0:T(8,128)S(1)}, f32[8,48,768]{2,1,0:T(8,128)}) custom-call(s32[1]{0:T(128)} %bitcast.mine_ref, f32[72,128]{1,0:T(8,128)S(1)} %get-tuple-element.83.coef_ref, f32[6,96,128]{2,1,0:T(8,128)S(1)} %bitcast.146, f32[6,96,128]{2,1,0:T(8,128)S(1)} %collective-permute-done.refs_1_, ...), custom_call_target="tpu_custom_call" | custom-call | flops 5435817984 | bytes 3538944 | tf_op jit(solution)/shard_map/pallas_call | solution.py:337
  145.8 9.5 %shard_map.46.refs_8_ = f32[768,768]{1,0:T(8,128)S(1)} custom-call(s32[1]{0:T(128)} %bitcast.mine_ref, f32[72,128]{1,0:T(8,128)S(1)} %get-tuple-element.80.coef_ref, f32[6,96,128]{2,1,0:T(8,128)S(1)} %bitcast.144, f32[6,96,128]{2,1,0:T(8,128)S(1)} %collective-permute-done.21.refs_1_.refs_5_, f32[6,96,128]{2,1,0:T(8,128)S(1)} %collective-permute-done.22.refs_2_.refs_6_, ...), custom_call_target="tpu_custom_call" | custom-call | flops 5435817984 | bytes 3538944 | tf_op jit(solution)/shard_map/pallas_call | solution.py:337
  160.2 8.7 %shard_map.47.refs_8_ = f32[768,768]{1,0:T(8,128)S(1)} custom-call(s32[1]{0:T(128)} %bitcast.mine_ref, f32[72,128]{1,0:T(8,128)S(1)} %get-tuple-element.81.coef_ref, f32[6,96,128]{2,1,0:T(8,128)S(1)} %bitcast.158, f32[6,96,128]{2,1,0:T(8,128)S(1)} %collective-permute-done.14.refs_1_.refs_5_, ...), custom_call_target="tpu_custom_call", output_to_operand_aliasing={{}: (10, {})} | custom-call | flops 5435817984 | bytes 3538944 | tf_op jit(solution)/shard_map/pallas_call | solution.py:337
  170.0 2.8 %collective-permute-start.6 = (f32[6,96,128]{2,1,0:T(8,128)S(1)}, f32[6,96,128]{2,1,0:T(8,128)S(1)}, u32[]{:S(2)}, u32[]{:S(2)}) collective-permute-start(f32[6,96,128]{2,1,0:T(8,128)S(1)} %collective-permute-done.2.refs_3_), channel_id=1, source_target_pairs={{0,28},{4,0},{8,4},{12,8},{16,12},{20,16},{24,20},{28,24},{1,29},{... | collective-permute-start | bytes 884744 | tf_op jit(solution)/shard_map/ppermute | solution.py:483
  172.8 8.7 %shard_map.48.refs_8_ = f32[768,768]{1,0:T(8,128)S(1)} custom-call(s32[1]{0:T(128)} %bitcast.mine_ref, f32[72,128]{1,0:T(8,128)S(1)} %get-tuple-element.82.coef_ref, f32[6,96,128]{2,1,0:T(8,128)S(1)} %bitcast.151, f32[6,96,128]{2,1,0:T(8,128)S(1)} %collective-permute-done.7.refs_1_.refs_5_, ...), custom_call_target="tpu_custom_call", output_to_operand_aliasing={{}: (10, {})} | custom-call | flops 5435817984 | bytes 3538944 | tf_op jit(solution)/shard_map/pallas_call | solution.py:337
  181.6 9.7 %shard_map.49 = (f32[8,48,768]{2,1,0:T(8,128)S(1)}, f32[8,48,768]{2,1,0:T(8,128)}) custom-call(s32[1]{0:T(128)} %bitcast.mine_ref, f32[72,128]{1,0:T(8,128)S(1)} %copy-done.3, f32[6,96,128]{2,1,0:T(8,128)S(1)} %bitcast.147, f32[6,96,128]{2,1,0:T(8,128)S(1)} %collective-permute-done.refs_1_, f32[6,96,128]{2,1,0:T(8,128)S(1)} %collective-permute-done.1.refs_2_, ...), custom_call_target="tpu_custom_call" | custom-call | flops 5435817984 | bytes 3538944 | tf_op jit(solution)/shard_map/pallas_call | solution.py:337
  208.4 2.4 collective-permute-done.42
  217.9 14.6 %collective-permute-done.43 = f32[2,48,768]{2,1,0:T(8,128)S(1)} collective-permute-done((f32[2,48,768]{2,1,0:T(8,128)S(1)}, f32[2,48,768]{2,1,0:T(8,128)S(1)}, u32[]{:S(2)}, u32[]{:S(2)}) %collective-permute-start.43) | collective-permute-done | bytes 294944 | tf_op jit(solution)/shard_map/ppermute | solution.py:422
  239.6 2.6 collective-permute-done.44
  243.3 2.5 collective-permute-start.45
  246.0 2.3 collective-permute-start.40
  250.0 4.9 %collective-permute-done.31 = f32[2,48,2,2,96]{4,3,2,1,0:T(2,128)S(1)} collective-permute-done((f32[2,48,2,2,96]{4,3,2,1,0:T(2,128)S(1)}, f32[2,48,2,2,96]{4,3,2,1,0:T(2,128)S(1)}, u32[]{:S(2)}, u32[]{:S(2)}) %collective-permute-start.31) | collective-permute-done | bytes 147488 | tf_op jit(solution)/shard_map/ppermute | solution.py:443
  256.0 5.5 %collective-permute-done.32 = f32[2,48,2,1,96]{4,2,1,0,3:T(2,128)S(1)} collective-permute-done((f32[2,48,2,1,96]{4,2,1,0,3:T(2,128)S(1)}, f32[2,48,2,1,96]{4,2,1,0,3:T(2,128)S(1)}, u32[]{:S(2)}, u32[]{:S(2)}) %collective-permute-start.32) | collective-permute-done | bytes 73760 | tf_op jit(solution)/shard_map/ppermute | solution.py:443
  (164 shorter events, 56.5 us)
Async XLA Ops:
  5.9 44.7 %collective-permute-start.21 = (f32[6,96,128]{2,1,0:T(8,128)S(1)}, f32[6,96,128]{2,1,0:T(8,128)S(1)}, u32[]{:S(2)}, u32[]{:S(2)}) collective-permute-start(f32[6,96,128]{2,1,0:T(8,128)S(1)} %bitcast.154), channel_id=1, source_target_pairs={{0,1},{1,0},{2,3},{3,2},{4,5},{5,4},{6,7},{7,6},{8,9},{9,8},{10,11... | collective-permute-start | bytes 884744 | tf_op jit(solution)/shard_map/ppermute | solution.py:459
  9.0 42.6 %collective-permute-start.22 = (f32[6,96,128]{2,1,0:T(8,128)S(1)}, f32[6,96,128]{2,1,0:T(8,128)S(1)}, u32[]{:S(2)}, u32[]{:S(2)}) collective-permute-start(f32[6,96,128]{2,1,0:T(8,128)S(1)} %bitcast.153), channel_id=1, source_target_pairs={{0,2},{1,3},{2,0},{3,1},{4,6},{5,7},{6,4},{7,5},{8,10},{9,11},{10,... | collective-permute-start | bytes 884744 | tf_op jit(solution)/shard_map/ppermute | solution.py:459
  11.6 41.6 %collective-permute-start.23 = (f32[6,96,128]{2,1,0:T(8,128)S(1)}, f32[6,96,128]{2,1,0:T(8,128)}, u32[]{:S(2)}, u32[]{:S(2)}) collective-permute-start(f32[6,96,128]{2,1,0:T(8,128)S(1)} %bitcast.152), channel_id=1, source_target_pairs={{0,3},{1,2},{2,1},{3,0},{4,7},{5,6},{6,5},{7,4},{8,11},{9,10},{10,... | collective-permute-start | bytes 884744 | tf_op jit(solution)/shard_map/ppermute | solution.py:459
  12.4 20.0 %collective-permute-start.33 = (f32[3,96,128]{2,1,0:T(8,128)}, f32[3,96,128]{2,1,0:T(8,128)S(1)}, u32[]{:S(2)}, u32[]{:S(2)}) collective-permute-start(f32[3,96,128]{2,1,0:T(8,128)} %pad_maximum_fusion.3), channel_id=1, source_target_pairs={{0,1},{1,0},{2,3},{3,2},{4,5},{5,4},{6,7},{7,6},{8,9},{9,8},{10,11... | collective-permute-start | bytes 442376 | tf_op jit(solution)/shard_map/ppermute | solution.py:459
  14.1 34.3 %collective-permute-start.34 = (f32[3,96,128]{2,1,0:T(8,128)}, f32[3,96,128]{2,1,0:T(8,128)}, u32[]{:S(2)}, u32[]{:S(2)}) collective-permute-start(f32[3,96,128]{2,1,0:T(8,128)} %pad_maximum_fusion.4), channel_id=1, source_target_pairs={{0,2},{1,3},{2,0},{3,1},{4,6},{5,7},{6,4},{7,5},{8,10},{9,11},{10,... | collective-permute-start | bytes 442376 | tf_op jit(solution)/shard_map/ppermute | solution.py:459
  32.4 16.0 %collective-permute-start.35 = (f32[3,96,128]{2,1,0:T(8,128)}, f32[3,96,128]{2,1,0:T(8,128)S(1)}, u32[]{:S(2)}, u32[]{:S(2)}) collective-permute-start(f32[3,96,128]{2,1,0:T(8,128)} %pad_maximum_fusion.5), channel_id=1, source_target_pairs={{0,3},{1,2},{2,1},{3,0},{4,7},{5,6},{6,5},{7,4},{8,11},{9,10},{10,... | collective-permute-start | bytes 442376 | tf_op jit(solution)/shard_map/ppermute | solution.py:459
  48.4 78.2 %collective-permute-start = (f32[6,96,128]{2,1,0:T(8,128)S(1)}, f32[6,96,128]{2,1,0:T(8,128)S(1)}, u32[]{:S(2)}, u32[]{:S(2)}) collective-permute-start(f32[6,96,128]{2,1,0:T(8,128)S(1)} %bitcast.161), channel_id=1, source_target_pairs={{0,1},{1,0},{2,3},{3,2},{4,5},{5,4},{6,7},{7,6},{8,9},{9,8},{10,11... | collective-permute-start | bytes 884744 | tf_op jit(solution)/shard_map/ppermute | solution.py:459
  48.4 21.1 %collective-permute-start.14 = (f32[6,96,128]{2,1,0:T(8,128)S(1)}, f32[6,96,128]{2,1,0:T(8,128)S(1)}, u32[]{:S(2)}, u32[]{:S(2)}) collective-permute-start(f32[6,96,128]{2,1,0:T(8,128)S(1)} %bitcast.167), channel_id=1, source_target_pairs={{0,1},{1,0},{2,3},{3,2},{4,5},{5,4},{6,7},{7,6},{8,9},{9,8},{10,11... | collective-permute-start | bytes 884744 | tf_op jit(solution)/shard_map/ppermute | solution.py:459
  50.6 18.8 %collective-permute-start.15 = (f32[6,96,128]{2,1,0:T(8,128)S(1)}, f32[6,96,128]{2,1,0:T(8,128)S(1)}, u32[]{:S(2)}, u32[]{:S(2)}) collective-permute-start(f32[6,96,128]{2,1,0:T(8,128)S(1)} %bitcast.166), channel_id=1, source_target_pairs={{0,2},{1,3},{2,0},{3,1},{4,6},{5,7},{6,4},{7,5},{8,10},{9,11},{10,... | collective-permute-start | bytes 884744 | tf_op jit(solution)/shard_map/ppermute | solution.py:459
  51.6 26.0 %collective-permute-start.16 = (f32[6,96,128]{2,1,0:T(8,128)S(1)}, f32[6,96,128]{2,1,0:T(8,128)S(1)}, u32[]{:S(2)}, u32[]{:S(2)}) collective-permute-start(f32[6,96,128]{2,1,0:T(8,128)S(1)} %bitcast.165), channel_id=1, source_target_pairs={{0,3},{1,2},{2,1},{3,0},{4,7},{5,6},{6,5},{7,4},{8,11},{9,10},{10,... | collective-permute-start | bytes 884744 | tf_op jit(solution)/shard_map/ppermute | solution.py:459
  53.2 90.4 %collective-permute-start.24 = (f32[6,96,128]{2,1,0:T(8,128)S(1)}, f32[6,96,128]{2,1,0:T(8,128)S(1)}, u32[]{:S(2)}, u32[]{:S(2)}) collective-permute-start(f32[6,96,128]{2,1,0:T(8,128)S(1)} %bitcast.141), channel_id=1, source_target_pairs={{0,28},{4,0},{8,4},{12,8},{16,12},{20,16},{24,20},{28,24},{1,29},{... | collective-permute-start | bytes 884744 | tf_op jit(solution)/shard_map/ppermute | solution.py:483
  69.4 22.9 %collective-permute-start.7 = (f32[6,96,128]{2,1,0:T(8,128)S(1)}, f32[6,96,128]{2,1,0:T(8,128)S(1)}, u32[]{:S(2)}, u32[]{:S(2)}) collective-permute-start(f32[6,96,128]{2,1,0:T(8,128)S(1)} %bitcast.164), channel_id=1, source_target_pairs={{0,1},{1,0},{2,3},{3,2},{4,5},{5,4},{6,7},{7,6},{8,9},{9,8},{10,11... | collective-permute-start | bytes 884744 | tf_op jit(solution)/shard_map/ppermute | solution.py:459
  69.4 41.7 %collective-permute-start.8 = (f32[6,96,128]{2,1,0:T(8,128)S(1)}, f32[6,96,128]{2,1,0:T(8,128)S(1)}, u32[]{:S(2)}, u32[]{:S(2)}) collective-permute-start(f32[6,96,128]{2,1,0:T(8,128)S(1)} %bitcast.163), channel_id=1, source_target_pairs={{0,2},{1,3},{2,0},{3,1},{4,6},{5,7},{6,4},{7,5},{8,10},{9,11},{10,... | collective-permute-start | bytes 884744 | tf_op jit(solution)/shard_map/ppermute | solution.py:459
  77.7 36.4 %collective-permute-start.9 = (f32[6,96,128]{2,1,0:T(8,128)S(1)}, f32[6,96,128]{2,1,0:T(8,128)S(1)}, u32[]{:S(2)}, u32[]{:S(2)}) collective-permute-start(f32[6,96,128]{2,1,0:T(8,128)S(1)} %bitcast.162), channel_id=1, source_target_pairs={{0,3},{1,2},{2,1},{3,0},{4,7},{5,6},{6,5},{7,4},{8,11},{9,10},{10,... | collective-permute-start | bytes 884744 | tf_op jit(solution)/shard_map/ppermute | solution.py:459
  92.4 36.8 %collective-permute-start.1 = (f32[6,96,128]{2,1,0:T(8,128)S(1)}, f32[6,96,128]{2,1,0:T(8,128)S(1)}, u32[]{:S(2)}, u32[]{:S(2)}) collective-permute-start(f32[6,96,128]{2,1,0:T(8,128)S(1)} %bitcast.160), channel_id=1, source_target_pairs={{0,2},{1,3},{2,0},{3,1},{4,6},{5,7},{6,4},{7,5},{8,10},{9,11},{10,... | collective-permute-start | bytes 884744 | tf_op jit(solution)/shard_map/ppermute | solution.py:459
  111.2 18.1 %collective-permute-start.2 = (f32[6,96,128]{2,1,0:T(8,128)S(1)}, f32[6,96,128]{2,1,0:T(8,128)S(1)}, u32[]{:S(2)}, u32[]{:S(2)}) collective-permute-start(f32[6,96,128]{2,1,0:T(8,128)S(1)} %bitcast.159), channel_id=1, source_target_pairs={{0,3},{1,2},{2,1},{3,0},{4,7},{5,6},{6,5},{7,4},{8,11},{9,10},{10,... | collective-permute-start | bytes 884744 | tf_op jit(solution)/shard_map/ppermute | solution.py:459
  114.1 67.4 %collective-permute-start.3 = (f32[6,96,128]{2,1,0:T(8,128)S(1)}, f32[6,96,128]{2,1,0:T(8,128)S(1)}, u32[]{:S(2)}, u32[]{:S(2)}) collective-permute-start(f32[6,96,128]{2,1,0:T(8,128)S(1)} %bitcast.145), channel_id=1, source_target_pairs={{0,28},{4,0},{8,4},{12,8},{16,12},{20,16},{24,20},{28,24},{1,29},{... | collective-permute-start | bytes 884744 | tf_op jit(solution)/shard_map/ppermute | solution.py:483
  126.6 17.1 %collective-permute-start.25 = (f32[6,96,128]{2,1,0:T(8,128)S(1)}, f32[6,96,128]{2,1,0:T(8,128)S(1)}, u32[]{:S(2)}, u32[]{:S(2)}) collective-permute-start(f32[6,96,128]{2,1,0:T(8,128)S(1)} %collective-permute-done.21.refs_1_.refs_5_), channel_id=1, source_target_pairs={{0,28},{4,0},{8,4},{12,8},{16,12},{20,16},{24,20},{28,24},{1,29},{... | collective-permute-start | bytes 884744 | tf_op jit(solution)/shard_map/ppermute | solution.py:483
  129.2 16.0 %collective-permute-start.26 = (f32[6,96,128]{2,1,0:T(8,128)S(1)}, f32[6,96,128]{2,1,0:T(8,128)S(1)}, u32[]{:S(2)}, u32[]{:S(2)}) collective-permute-start(f32[6,96,128]{2,1,0:T(8,128)S(1)} %collective-permute-done.22.refs_2_.refs_6_), channel_id=1, source_target_pairs={{0,28},{4,0},{8,4},{12,8},{16,12},{20,16},{24,20},{28,24},{1,29},{... | collective-permute-start | bytes 884744 | tf_op jit(solution)/shard_map/ppermute | solution.py:483
  129.3 16.0 %collective-permute-start.27 = (f32[6,96,128]{2,1,0:T(8,128)}, f32[6,96,128]{2,1,0:T(8,128)S(1)}, u32[]{:S(2)}, u32[]{:S(2)}) collective-permute-start(f32[6,96,128]{2,1,0:T(8,128)} %collective-permute-done.23.refs_3_.refs_7_), channel_id=1, source_target_pairs={{0,28},{4,0},{8,4},{12,8},{16,12},{20,16},{24,20},{28,24},{1,29},{... | collective-permute-start | bytes 884744 | tf_op jit(solution)/shard_map/ppermute | solution.py:483
  145.1 12.8 %collective-permute-start.19 = (f32[6,96,128]{2,1,0:T(8,128)S(1)}, f32[6,96,128]{2,1,0:T(8,128)S(1)}, u32[]{:S(2)}, u32[]{:S(2)}) collective-permute-start(f32[6,96,128]{2,1,0:T(8,128)S(1)} %collective-permute-done.15.refs_2_.refs_6_), channel_id=1, source_target_pairs={{0,28},{4,0},{8,4},{12,8},{16,12},{20,16},{24,20},{28,24},{1,29},{... | collective-permute-start | bytes 884744 | tf_op jit(solution)/shard_map/ppermute | solution.py:483
  145.2 13.0 %collective-permute-start.20 = (f32[6,96,128]{2,1,0:T(8,128)S(1)}, f32[6,96,128]{2,1,0:T(8,128)S(1)}, u32[]{:S(2)}, u32[]{:S(2)}) collective-permute-start(f32[6,96,128]{2,1,0:T(8,128)S(1)} %collective-permute-done.16.refs_3_.refs_7_), channel_id=1, source_target_pairs={{0,28},{4,0},{8,4},{12,8},{16,12},{20,16},{24,20},{28,24},{1,29},{... | collective-permute-start | bytes 884744 | tf_op jit(solution)/shard_map/ppermute | solution.py:483
  155.3 13.6 %collective-permute-start.10 = (f32[6,96,128]{2,1,0:T(8,128)S(1)}, f32[6,96,128]{2,1,0:T(8,128)S(1)}, u32[]{:S(2)}, u32[]{:S(2)}) collective-permute-start(f32[6,96,128]{2,1,0:T(8,128)S(1)} %bitcast.150), channel_id=1, source_target_pairs={{0,28},{4,0},{8,4},{12,8},{16,12},{20,16},{24,20},{28,24},{1,29},{... | collective-permute-start | bytes 884744 | tf_op jit(solution)/shard_map/ppermute | solution.py:483
  155.6 13.4 %collective-permute-start.11 = (f32[6,96,128]{2,1,0:T(8,128)S(1)}, f32[6,96,128]{2,1,0:T(8,128)S(1)}, u32[]{:S(2)}, u32[]{:S(2)}) collective-permute-start(f32[6,96,128]{2,1,0:T(8,128)S(1)} %collective-permute-done.7.refs_1_.refs_5_), channel_id=1, source_target_pairs={{0,28},{4,0},{8,4},{12,8},{16,12},{20,16},{24,20},{28,24},{1,29},{... | collective-permute-start | bytes 884744 | tf_op jit(solution)/shard_map/ppermute | solution.py:483
  168.9 23.0 %collective-permute-start.41 = (f32[8,48,768]{2,1,0:T(8,128)}, f32[8,48,768]{2,1,0:T(8,128)}, u32[]{:S(2)}, u32[]{:S(2)}) collective-permute-start(f32[8,48,768]{2,1,0:T(8,128)} %get-tuple-element.56), channel_id=1, source_target_pairs={{0,4},{4,0},{8,12},{12,8},{16,20},{20,16},{24,28},{28,24},{1,5},{5... | collective-permute-start | bytes 3538952 | tf_op jit(solution)/shard_map/ppermute | solution.py:430
  181.5 14.5 %collective-permute-start.36 = (f32[8,48,768]{2,1,0:T(8,128)}, f32[8,48,768]{2,1,0:T(8,128)}, u32[]{:S(2)}, u32[]{:S(2)}) collective-permute-start(f32[8,48,768]{2,1,0:T(8,128)} %get-tuple-element.54), channel_id=1, source_target_pairs={{0,4},{4,0},{8,12},{12,8},{16,20},{20,16},{24,28},{28,24},{1,5},{5... | collective-permute-start | bytes 3538952 | tf_op jit(solution)/shard_map/ppermute | solution.py:430
  191.4 14.4 %collective-permute-start.28 = (f32[8,48,768]{2,1,0:T(8,128)}, f32[8,48,768]{2,1,0:T(8,128)}, u32[]{:S(2)}, u32[]{:S(2)}) collective-permute-start(f32[8,48,768]{2,1,0:T(8,128)} %get-tuple-element.48), channel_id=1, source_target_pairs={{0,4},{4,0},{8,12},{12,8},{16,20},{20,16},{24,28},{28,24},{1,5},{5... | collective-permute-start | bytes 3538952 | tf_op jit(solution)/shard_map/ppermute | solution.py:430
  195.2 15.6 %collective-permute-start.42 = (f32[2,2,48,768]{3,2,1,0:T(8,128)}, f32[2,2,48,768]{3,2,1,0:T(8,128)}, u32[]{:S(2)}, u32[]{:S(2)}) collective-permute-start(f32[2,2,48,768]{3,2,1,0:T(8,128)} %dynamic-slice_bitcast_fusion), channel_id=1, source_target_pairs={{0,16},{4,20},{8,24},{12,28},{16,0},{20,4},{24,8},{28,12},{1,17},{... | collective-permute-start | bytes 1769480 | tf_op jit(solution)/shard_map/ppermute | solution.py:422
  198.4 16.5 %collective-permute-start.37 = (f32[2,2,48,768]{3,2,1,0:T(8,128)}, f32[2,2,48,768]{3,2,1,0:T(8,128)}, u32[]{:S(2)}, u32[]{:S(2)}) collective-permute-start(f32[2,2,48,768]{3,2,1,0:T(8,128)} %dynamic-slice_bitcast_fusion.1), channel_id=1, source_target_pairs={{0,8},{4,12},{8,0},{12,4},{16,24},{20,28},{24,16},{28,20},{1,9},{5... | collective-permute-start | bytes 1769480 | tf_op jit(solution)/shard_map/ppermute | solution.py:422
  207.2 29.9 %collective-permute-start.29 = (f32[2,2,48,768]{3,2,1,0:T(8,128)S(1)}, f32[2,2,48,768]{3,2,1,0:T(8,128)}, u32[]{:S(2)}, u32[]{:S(2)}) collective-permute-start(f32[2,2,48,768]{3,2,1,0:T(8,128)S(1)} %dynamic-slice_bitcast_fusion.2), channel_id=1, source_target_pairs={{0,8},{4,12},{8,0},{12,4},{16,24},{20,28},{24,16},{28,20},{1,9},{5... | collective-permute-start | bytes 1769480 | tf_op jit(solution)/shard_map/ppermute | solution.py:422
  212.0 20.6 %collective-permute-start.43 = (f32[2,48,768]{2,1,0:T(8,128)S(1)}, f32[2,48,768]{2,1,0:T(8,128)S(1)}, u32[]{:S(2)}, u32[]{:S(2)}) collective-permute-start(f32[2,48,768]{2,1,0:T(8,128)S(1)} %dynamic-slice_bitcast_fusion.3), channel_id=1, source_target_pairs={{0,8},{4,12},{8,0},{12,4},{16,24},{20,28},{24,16},{28,20},{1,9},{5... | collective-permute-start | bytes 884744 | tf_op jit(solution)/shard_map/ppermute | solution.py:422
  216.8 18.8 %collective-permute-start.38 = (f32[2,48,768]{2,1,0:T(8,128)}, f32[2,48,768]{2,1,0:T(8,128)S(1)}, u32[]{:S(2)}, u32[]{:S(2)}) collective-permute-start(f32[2,48,768]{2,1,0:T(8,128)} %dynamic-slice_bitcast_fusion.4), channel_id=1, source_target_pairs={{0,16},{4,20},{8,24},{12,28},{16,0},{20,4},{24,8},{28,12},{1,17},{... | collective-permute-start | bytes 884744 | tf_op jit(solution)/shard_map/ppermute | solution.py:422
  (27 other events, 321.6 us)
